TPU v7x, 32 devices: a whole 2x2x4 slice. The times are simulated.
32 devices in a mesh: gx: 4 (over y, x), gy: 2 (over core), gz: 4 (over z).
Axes of the slice: x: 2, y: 2, z: 4, core: 2. Of those that a mesh axis runs over, the one named last changes fastest.
Arguments:
- velocity: float32 [3, 2621440], P(None, ('gx', 'gy', 'gz')), may hold values from -6 to 6
- particle_place: int32 [2621440], P(('gx', 'gy', 'gz')), may hold values from 0 to 8191
- grid_shift: int32 [3], replicated, may hold values from 1 to 3
- rotation_axis: int32 [64, 128, 64], P('gy', 'gx', 'gz'), may hold values from 0 to 1023
Outputs:
- new_velocity: float32 [3, 2621440], P(None, ('gx', 'gy', 'gz'))
- modes: float32 [2, 3, 64, 64, 128], P(None, None, ('gy', 'gz'), 'gx')
- spectrum: float32 [32], replicated
Inputs may be any that keep to these rules, and one draw needn't show every extreme that they name: `particle_place`: A device's particle slots come in tiles of 640 slots; tile j holds particles of the device's local cells j * 128 to j * 128 + 127, and a value is (cell within the tile) * 4**3 + (sub-cell code).
All inputs are finite; a program needn't handle non-finite values.
Results may differ from a plain program's by a relative error of at most 0.0005.
Values sent between devices are 32-bit elements; how exact they have to be, the bound alone decides.
A program may use at most 128 MiB of HBM per device.

v0:
```python
import functools
import math

import jax
import jax.numpy as jnp
from jax import lax
from jax.experimental import pallas as pl
from jax.experimental.pallas import tpu as pltpu
from jax.sharding import PartitionSpec as P

PPC = 5
TILE = 128
SUB = 4
NAXES = 1024

ROT_COS = math.cos(130.0 * math.pi / 180.0)
ROT_SIN = math.sin(130.0 * math.pi / 180.0)
HIGH = lax.Precision.HIGHEST
F32 = jnp.float32
VMEM = pltpu.VMEM


def iota(shape, dim):
    return lax.broadcasted_iota(jnp.int32, shape, dim)


def shift_bits(place, shift_ref):
    code = place & (SUB**3 - 1)
    bit_x = jnp.where((code >> 4) + shift_ref[0] >= SUB, 1, 0)
    bit_y = jnp.where(((code >> 2) & 3) + shift_ref[1] >= SUB, 1, 0)
    bit_z = jnp.where((code & 3) + shift_ref[2] >= SUB, 1, 0)
    return bit_x, bit_y, bit_z


def deposit_kernel(shift_ref, place_ref, v_ref, out_ref):
    place = place_ref[...]
    bit_x, bit_y, bit_z = shift_bits(place, shift_ref)
    octant = bit_x * 4 + bit_y * 2 + bit_z
    member = place >> 6
    sub8 = iota((8, TILE), 0)
    cells = iota((TILE, TILE), 0)
    for tile in range(8):
        lhs = []
        hots = []
        for chunk in range(PPC):
            row = tile * PPC + chunk
            mask = jnp.broadcast_to(octant[row : row + 1], (8, TILE)) == sub8
            parts = []
            for c in range(3):
                value = v_ref[c : c + 1, row * TILE : (row + 1) * TILE]
                high = value.astype(jnp.bfloat16).astype(F32)
                low = value - high
                for part in (high, low):
                    parts.append(jnp.where(mask, jnp.broadcast_to(part, (8, TILE)), 0.0))
            parts.append(jnp.where(mask, 1.0, 0.0))
            parts.append(jnp.zeros((8, TILE), F32))
            lhs.append(jnp.concatenate(parts, axis=0).astype(jnp.bfloat16))
            hot = jnp.broadcast_to(member[row : row + 1], (TILE, TILE)) == cells
            hots.append(jnp.where(hot, 1.0, 0.0).astype(jnp.bfloat16))
        sums = lax.dot_general(
            jnp.concatenate(lhs, axis=1),
            jnp.concatenate(hots, axis=1),
            (((1,), (1,)), ((), ())),
            preferred_element_type=F32,
        )
        for c in range(3):
            out_ref[c, :, tile, :] = sums[16 * c : 16 * c + 8] + sums[16 * c + 8 : 16 * c + 16]
        out_ref[3, :, tile, :] = sums[48:56]


def axis_vectors(index):
    level = 1.0 - (2.0 * index + 1.0) / NAXES
    radius = jnp.sqrt(1.0 - level * level)
    steps = index.astype(jnp.int32) * 1597 % 2584
    turn = steps.astype(F32) * (2.0 * math.pi / 2584.0)
    return radius * jnp.cos(turn), radius * jnp.sin(turn), level


def rotate(offset, n):
    along = (n[0] * offset[0] + n[1] * offset[1] + n[2] * offset[2]) * (1.0 - ROT_COS)
    cross = (
        n[1] * offset[2] - n[2] * offset[1],
        n[2] * offset[0] - n[0] * offset[2],
        n[0] * offset[1] - n[1] * offset[0],
    )
    return [ROT_COS * offset[c] + ROT_SIN * cross[c] + along * n[c] for c in range(3)]


def roll(x, amount, dim=1):
    amount = amount % x.shape[dim]
    return pltpu.roll(x, amount, dim) if amount else x


def take(x, index):
    return jnp.take_along_axis(x, index, axis=1)


def neighbours(name):
    count = lax.axis_size(name)
    me = lax.axis_index(name)
    return lax.rem(me + 1, count), lax.rem(me + count - 1, count)


def halo_kernel(
    s_ref, a_ref, tab_ref, cell_ref,
    y_low, y_up, ya_up, grid_sums, axis_ext, xs, face_sums,
    x_send_up, x_send_down, x_low, x_up, z_send_up, z_send_down, z_low, z_up,
    total, work, tables, send_sem, recv_sem,
):
    rows = 136
    lane = iota((8, TILE), 1)
    sub = iota((8, TILE), 0)
    lane_z = lane & 15

    barrier = pltpu.get_barrier_semaphore()
    for name in ("gx", "gy", "gz"):
        for side in neighbours(name):
            pl.semaphore_signal(
                barrier, inc=1, device_id={name: side}, device_id_type=pl.DeviceIdType.MESH
            )
    pl.semaphore_wait(barrier, 6)

    def remote(src, dst, name, upward, slot):
        up, down = neighbours(name)
        return pltpu.make_async_remote_copy(
            src_ref=src, dst_ref=dst, send_sem=send_sem.at[slot], recv_sem=recv_sem.at[slot],
            device_id={name: up if upward else down}, device_id_type=pl.DeviceIdType.MESH,
        )

    copies = [
        remote(s_ref.at[:, :, 1, :, pl.ds(120, 8), :], y_low, "gy", True, 0),
        remote(s_ref.at[:, :, 0, :, pl.ds(0, 8), :], y_up, "gy", False, 1),
        remote(a_ref.at[pl.ds(0, 8), :], ya_up, "gy", False, 2),
    ]
    for copy in copies:
        copy.start()
    for q in range(4):
        for bx in range(2):
            for bz in range(2):
                grid_sums[q, bx, bz, 8:128, :] = (
                    s_ref[q, bx, 0, bz, 8:128, :] + s_ref[q, bx, 1, bz, 4:124, :]
                )
    axis_ext[0:128, :] = a_ref[...]
    for copy in copies:
        copy.wait()
    for q in range(4):
        for bx in range(2):
            for bz in range(2):
                grid_sums[q, bx, bz, 0:8, :] = s_ref[q, bx, 0, bz, 0:8, :] + jnp.where(
                    sub < 4,
                    roll(y_low[q, bx, bz], 4, 0),
                    roll(s_ref[q, bx, 1, bz, 0:8, :], 4, 0),
                )
                grid_sums[q, bx, bz, 128:136, :] = jnp.where(
                    sub < 4,
                    roll(s_ref[q, bx, 1, bz, 120:128, :], 4, 0) + y_up[q, bx, bz],
                    0.0,
                )
    axis_ext[128:136, :] = jnp.where(sub < 4, ya_up[...], 0.0)

    lane40 = iota((40, TILE), 1)
    zeros40 = jnp.zeros((40, TILE), F32)
    pack_up = zeros40
    pack_down = zeros40
    fill = jnp.zeros((6, TILE), F32)
    for q in range(4):
        for bz in range(2):
            i = q * 2 + bz
            xs[i, 0:8, :] = jnp.zeros((8, TILE), F32)
            xs[i, 136:144, :] = jnp.zeros((8, TILE), F32)
            xs[i, 1:137, :] = roll(grid_sums[q, 1, bz], 16)
            up_rows = jnp.concatenate([xs[i, pl.ds(4, 34, stride=4), :], fill], axis=0)
            down_rows = jnp.concatenate([grid_sums[q, 0, bz, pl.ds(0, 34, stride=4), :], fill], axis=0)
            slot = (lane40 >> 4) == i
            pack_up = jnp.where(slot, roll(up_rows, 16 * i), pack_up)
            pack_down = jnp.where(slot, roll(down_rows, 16 * i), pack_down)
    x_send_up[...] = pack_up
    x_send_down[0] = pack_down
    x_send_down[1] = jnp.concatenate([axis_ext[pl.ds(0, 34, stride=4), :], fill], axis=0)
    copies = [
        remote(x_send_up, x_low, "gx", True, 3),
        remote(x_send_down, x_up, "gx", False, 4),
    ]
    for copy in copies:
        copy.start()
    for copy in copies:
        copy.wait()
    lane_r = iota((rows, TILE), 1)
    from_low = x_low[...]
    for q in range(4):
        for bz in range(2):
            i = q * 2 + bz
            ring = roll(grid_sums[q, 1, bz], 16)
            xs[i, pl.ds(0, 34, stride=4), :] = roll(from_low, -16 * i)[0:34]
            face_sums[q, bz] = grid_sums[q, 0, bz] + jnp.where(lane_r >= 16, ring, xs[i, 0:136, :])
    x32 = pack_up + x_up[0]
    ax32 = x_up[1]

    def squeeze(load, z_pos):
        first = jnp.zeros((8, TILE), F32)
        for k in range(16):
            first = jnp.where(lane_z == k, roll(load(8 * k), k - z_pos), first)
        second = roll(load(128), -z_pos)
        return first, second

    def squeeze_edge(value, from_lane):
        out = jnp.zeros((8, TILE), F32)
        for g in range(5):
            out = jnp.where((lane & 31) == g, roll(value[8 * g : 8 * g + 8], g - from_lane), out)
        return out

    for q in range(4):
        z_send_up[q], z_send_up[4 + q] = squeeze(lambda r: face_sums[q, 1, r : r + 8, :], 15)
        z_send_down[q], z_send_down[4 + q] = squeeze(lambda r: face_sums[q, 0, r : r + 8, :], 0)
    z_send_up[8] = squeeze_edge(x32, 31)
    z_send_down[8] = squeeze_edge(x32, 0)
    z_send_down[9], z_send_down[10] = squeeze(lambda r: axis_ext[r : r + 8, :], 0)
    z_send_down[11] = squeeze_edge(ax32, 0)
    copies = [
        remote(z_send_up, z_low, "gz", True, 5),
        remote(z_send_down, z_up, "gz", False, 6),
    ]
    for copy in copies:
        copy.start()
    for copy in copies:
        copy.wait()

    def spread(buf, q, k):
        return roll(buf[q], -k) if k < 16 else buf[4 + q]

    for q in range(4):
        for k in range(17):
            r = 8 * k
            one = face_sums[q, 1, r : r + 8, :]
            total[0, q, r : r + 8, :] = face_sums[q, 0, r : r + 8, :] + jnp.where(
                lane_z == 0, spread(z_low, q, k), roll(one, 1)
            )
            total[1, q, r : r + 8, :] = roll(one, -15) + spread(z_up, q, k)
    edge = []
    ax_edge = []
    for g in range(5):
        one = x32[8 * g : 8 * g + 8]
        part = lane & 31
        main = one + jnp.where(part == 0, roll(z_low[8], -g), roll(one, -15))
        last = roll(one, -15) + roll(z_up[8], 16 - g)
        edge.append(jnp.where(part == 16, last, main))
        ax_edge.append(jnp.where(lane == 16, roll(z_up[11], 16 - g), ax32[8 * g : 8 * g + 8]))
    edge = jnp.concatenate(edge, axis=0)
    ax_edge = jnp.concatenate(ax_edge, axis=0)

    edge_count = jnp.maximum(roll(edge, -96), 1.0)
    scale = [1.0 / jnp.maximum(total[f, 3], 1.0) for f in range(2)]
    axis_top = jnp.concatenate(
        [roll(z_up[9], -k) for k in range(16)] + [z_up[10]], axis=0
    )
    pick = jnp.clip(lane_r - 32, 0, 7) * 16
    for c in range(4):
        if c < 3:
            inner = total[0, c] * scale[0]
            top = total[1, c] * scale[1]
            side = roll(edge, -32 * c) / edge_count
        else:
            inner, top, side = axis_ext[...], axis_top, ax_edge
        work[0:136, :] = jnp.where(lane_r < 16, inner, roll(top, 16))
        work[136:144, :] = jnp.zeros((8, TILE), F32)
        work[pl.ds(4, 34, stride=4), :] = side[0:34]
        rim = jnp.where(lane_r <= 16, work[1:137, :], take(top, pick))
        if c < 3:
            tables[0, c] = inner
            tables[1, c] = rim
        else:
            in_range = jnp.where((lane_r <= 16) | ((lane_r >= 32) & (lane_r < 40)), rim, 0.0)
            for f, value in enumerate((inner, in_range)):
                for d, vec in enumerate(axis_vectors(value)):
                    tables[f, 3 + d] = vec
    for by in range(2):
        tab_ref[by] = tables[:, :, 4 * by : 4 * by + 128, :]

    xl = lane >> 4

    @pl.loop(0, 16)
    def _(k):
        r = pl.multiple_of(k * 8, 8)
        sums = [jnp.zeros((8, TILE), F32) for _ in range(3)]
        number = jnp.zeros((8, TILE), F32)
        for bx in range(2):
            for bz in range(2):
                x_new, z_new = xl + bx, lane_z + bz
                outside = (x_new == 8) | (z_new == 16)
                rim_at = jnp.where(x_new == 8, z_new, 32 + x_new)
                index = jnp.where(outside, rim_at, (lane + 16 * bx + bz) & 127)
                for by in range(2):
                    got = []
                    for c in range(6):
                        main = tab_ref[by, 0, c, pl.ds(r, 8), :]
                        if bx or bz:
                            rim = tab_ref[by, 1, c, pl.ds(r, 8), :]
                            main = jnp.where(outside, take(rim, index), take(main, index))
                        got.append(main)
                    count = s_ref[3, bx, by, bz, pl.ds(r, 8), :]
                    number = number + count
                    drift = [count * got[c] for c in range(3)]
                    offset = [s_ref[c, bx, by, bz, pl.ds(r, 8), :] - drift[c] for c in range(3)]
                    turned = rotate(offset, got[3:6])
                    sums = [sums[c] + drift[c] + turned[c] for c in range(3)]
        inverse = 1.0 / jnp.maximum(number, 1.0)
        for c in range(3):
            cell_ref[c, pl.ds(r, 8), :] = sums[c] * inverse


def collide_kernel(shift_ref, place_ref, v_ref, tab_ref, out_ref):
    sub = iota((8, TILE), 0)
    for chunk in range(PPC):
        place = place_ref[pl.ds(chunk, 8, stride=PPC), :]
        bit_x, bit_y, bit_z = shift_bits(place, shift_ref)
        cell = place >> 6
        x_new = (cell >> 4) + bit_x
        z_new = (cell & 15) + bit_z
        outside = (x_new == 8) | (z_new == 16)
        rim_at = jnp.where(x_new == 8, z_new, 32 + x_new)
        index = jnp.where(outside, rim_at, (cell + 16 * bit_x + bit_z) & 127)
        upper = bit_y == 1
        got = []
        for c in range(6):
            low = jnp.where(outside, take(tab_ref[0, 1, c], index), take(tab_ref[0, 0, c], index))
            high = jnp.where(outside, take(tab_ref[1, 1, c], index), take(tab_ref[1, 0, c], index))
            got.append(jnp.where(upper, high, low))
        speed = []
        for c in range(3):
            value = jnp.zeros((8, TILE), F32)
            for tile in range(8):
                at = (tile * PPC + chunk) * TILE
                value = jnp.where(
                    sub == tile, jnp.broadcast_to(v_ref[c : c + 1, at : at + TILE], (8, TILE)), value
                )
            speed.append(value)
        turned = rotate([speed[c] - got[c] for c in range(3)], got[3:6])
        for c in range(3):
            value = got[c] + turned[c]
            for tile in range(8):
                at = (tile * PPC + chunk) * TILE
                out_ref[c : c + 1, at : at + TILE] = value[tile : tile + 1]


def deposit(grid_shift, place, velocity, tiles):
    rows = 8 * PPC
    return pl.pallas_call(
        deposit_kernel,
        grid=(tiles // 8,),
        in_specs=[
            pl.BlockSpec(memory_space=pltpu.SMEM),
            pl.BlockSpec((rows, TILE), lambda i: (i, 0)),
            pl.BlockSpec((3, rows * TILE), lambda i: (0, i)),
        ],
        out_specs=pl.BlockSpec((4, 8, 8, TILE), lambda i: (0, 0, i, 0)),
        out_shape=jax.ShapeDtypeStruct((4, 8, tiles, TILE), F32),
        name="deposit",
    )(grid_shift, place, velocity)


def halo(sums, axis, tiles):
    dma = pltpu.SemaphoreType.DMA
    return pl.pallas_call(
        halo_kernel,
        in_specs=[pl.BlockSpec(memory_space=VMEM)] * 2,
        out_specs=[pl.BlockSpec(memory_space=VMEM)] * 2,
        out_shape=[
            jax.ShapeDtypeStruct((2, 2, 6, tiles, TILE), F32),
            jax.ShapeDtypeStruct((3, tiles, TILE), F32),
        ],
        scratch_shapes=[
            VMEM((4, 2, 2, 8, TILE), F32),
            VMEM((4, 2, 2, 8, TILE), F32),
            VMEM((8, TILE), F32),
            VMEM((4, 2, 2, 136, TILE), F32),
            VMEM((136, TILE), F32),
            VMEM((8, 144, TILE), F32),
            VMEM((4, 2, 136, TILE), F32),
            VMEM((40, TILE), F32),
            VMEM((2, 40, TILE), F32),
            VMEM((40, TILE), F32),
            VMEM((2, 40, TILE), F32),
            VMEM((9, 8, TILE), F32),
            VMEM((12, 8, TILE), F32),
            VMEM((9, 8, TILE), F32),
            VMEM((12, 8, TILE), F32),
            VMEM((2, 4, 136, TILE), F32),
            VMEM((144, TILE), F32),
            VMEM((2, 6, 136, TILE), F32),
            dma((7,)),
            dma((7,)),
        ],
        compiler_params=pltpu.CompilerParams(collective_id=0, has_side_effects=True),
        name="halo",
    )(sums, axis)


def collide_particles(grid_shift, place, velocity, tables, tiles):
    rows = 8 * PPC
    return pl.pallas_call(
        collide_kernel,
        grid=(tiles // 8,),
        in_specs=[
            pl.BlockSpec(memory_space=pltpu.SMEM),
            pl.BlockSpec((rows, TILE), lambda i: (i, 0)),
            pl.BlockSpec((3, rows * TILE), lambda i: (0, i)),
            pl.BlockSpec((2, 2, 6, 8, TILE), lambda i: (0, 0, 0, i, 0)),
        ],
        out_specs=pl.BlockSpec((3, rows * TILE), lambda i: (0, i)),
        out_shape=jax.ShapeDtypeStruct(velocity.shape, F32),
        cost_estimate=pl.CostEstimate(flops=60 * velocity.size, bytes_accessed=4000000, transcendentals=0),
        name="collide",
    )(grid_shift, place, velocity, tables)


def phase_tables(positions, length):
    phase_step = positions[..., None] * jnp.arange(length, dtype=jnp.int32) % length
    angle = phase_step.astype(jnp.float32) * (2.0 * math.pi / length)
    return (jnp.cos(angle), jnp.sin(angle))


def signed_wave(first_wave, count_here, length):
    wave = first_wave + jnp.arange(count_here, dtype=jnp.int32)
    return jnp.where(wave >= length // 2, wave - length, wave)


def per_device(velocity, particle_place, grid_shift, rotation_axis):
    size_y, size_x, size_z = rotation_axis.shape
    cell_count = size_y * size_x * size_z
    tile_count = cell_count // TILE
    place = particle_place.reshape(tile_count * PPC, TILE)
    sums = deposit(grid_shift, place, velocity, tile_count)
    axis = rotation_axis.reshape(tile_count, TILE).astype(F32)
    tables, cell_sums = halo(sums.reshape(4, 2, 2, 2, tile_count, TILE), axis, tile_count)
    new_velocity = collide_particles(grid_shift, place, velocity, tables, tile_count)
    cell_velocity = cell_sums.reshape(3, cell_count)
    count_x = lax.axis_size("gx")
    count_y = lax.axis_size("gy")
    count_z = lax.axis_size("gz")
    rows_y = size_y // count_z
    length_x = size_x * count_x
    length_y = size_y * count_y
    length_z = size_z * count_z
    arrived = lax.all_to_all(cell_velocity, "gz", split_axis=1, concat_axis=0, tiled=True)
    arrived = arrived.reshape(count_z, 3, rows_y, size_x, size_z)
    position_z = (
        jnp.arange(count_z, dtype=jnp.int32)[:, None] * size_z
        + jnp.arange(size_z, dtype=jnp.int32)[None, :]
    )
    cos_z, sin_z = phase_tables(position_z, length_z)
    real_z = jnp.einsum("gcyxz,gzk->kcyx", arrived, cos_z, precision=HIGH)
    imag_z = -jnp.einsum("gcyxz,gzk->kcyx", arrived, sin_z, precision=HIGH)
    stacked_z = jnp.stack([real_z, imag_z], axis=1).reshape(length_z, 6, rows_y * size_x)
    pencil = lax.all_to_all(stacked_z, ("gy", "gz"), split_axis=0, concat_axis=1, tiled=True)
    outer_count, outer_step, inner_count, inner_step = (count_y, size_y, count_z, rows_y)
    depth_z = length_z // (count_y * count_z)
    pencil = pencil.reshape(depth_z, outer_count, inner_count, 2, 3, rows_y, size_x)
    position_y = (
        jnp.arange(outer_count, dtype=jnp.int32)[:, None, None] * outer_step
        + jnp.arange(inner_count, dtype=jnp.int32)[None, :, None] * inner_step
        + jnp.arange(rows_y, dtype=jnp.int32)[None, None, :]
    )
    cos_y, sin_y = phase_tables(position_y, length_y)
    part_re = pencil[:, :, :, 0]
    part_im = pencil[:, :, :, 1]
    real_y = jnp.einsum("zabcyx,abyk->kzcx", part_re, cos_y, precision=HIGH) + jnp.einsum(
        "zabcyx,abyk->kzcx", part_im, sin_y, precision=HIGH
    )
    imag_y = jnp.einsum("zabcyx,abyk->kzcx", part_im, cos_y, precision=HIGH) - jnp.einsum(
        "zabcyx,abyk->kzcx", part_re, sin_y, precision=HIGH
    )
    stacked_y = jnp.stack([real_y, imag_y], axis=2).reshape(length_y, depth_z * 6 * size_x)
    columns = lax.all_to_all(stacked_y, "gx", split_axis=0, concat_axis=1, tiled=True)
    depth_y = length_y // count_x
    columns = columns.reshape(depth_y, count_x, depth_z, 2, 3, size_x)
    position_x = (
        jnp.arange(count_x, dtype=jnp.int32)[:, None] * size_x
        + jnp.arange(size_x, dtype=jnp.int32)[None, :]
    )
    cos_x, sin_x = phase_tables(position_x, length_x)
    col_re = columns[:, :, :, 0]
    col_im = columns[:, :, :, 1]
    real_x = jnp.einsum("ygzcx,gxk->czyk", col_re, cos_x, precision=HIGH) + jnp.einsum(
        "ygzcx,gxk->czyk", col_im, sin_x, precision=HIGH
    )
    imag_x = jnp.einsum("ygzcx,gxk->czyk", col_im, cos_x, precision=HIGH) - jnp.einsum(
        "ygzcx,gxk->czyk", col_re, sin_x, precision=HIGH
    )
    norm_scale = 1.0 / math.sqrt(length_x * length_y * length_z)
    modes = jnp.stack([real_x, imag_x], axis=0) * norm_scale
    energy = jnp.sum(modes * modes, axis=(0, 1))
    first_z = (lax.axis_index("gy") * count_z + lax.axis_index("gz")) * depth_z
    first_y = lax.axis_index("gx") * depth_y
    wave_z = signed_wave(first_z, depth_z, length_z)
    wave_y = signed_wave(first_y, depth_y, length_y)
    wave_x = signed_wave(0, length_x, length_x)
    square = wave_z[:, None, None] ** 2 + wave_y[None, :, None] ** 2 + wave_x[None, None, :] ** 2
    shell_index = jnp.floor(jnp.sqrt(square.astype(jnp.float32))).astype(jnp.int32)
    shells = min(min(length_x, length_y), length_z) // 2
    ladder = jnp.arange(shells, dtype=jnp.int32)

    def bin_plane(plane_pair):
        plane_energy, plane_shell = plane_pair
        member_shell = (plane_shell[..., None] == ladder).astype(jnp.float32)
        return (
            jnp.einsum("yx,yxs->s", plane_energy, member_shell, precision=HIGH),
            jnp.sum(member_shell, axis=(0, 1)),
        )

    plane_sums, plane_counts = lax.map(bin_plane, (energy, shell_index))
    shell_totals = lax.psum(
        (jnp.sum(plane_sums, axis=0), jnp.sum(plane_counts, axis=0)), ("gx", "gy", "gz")
    )
    spectrum = shell_totals[0] / shell_totals[1]
    return (new_velocity, modes, spectrum)


def solution(mesh):
    placed = (P(None, ("gx", "gy", "gz")), P(("gx", "gy", "gz")), P(), P("gy", "gx", "gz"))
    return jax.shard_map(
        per_device,
        mesh=mesh,
        in_specs=placed,
        out_specs=(P(None, ("gx", "gy", "gz")), P(None, None, ("gy", "gz"), "gx", None), P()),
        check_vma=False,
    )
```

profile of v0, /device:TPU:0, one launch (start us, length us, event | category | flops | bytes accessed | tf_op | source)
XLA Modules:
  0.0 149.2 jit_solution(6768244465224609030)
XLA Ops:
  0.6 1.0 convert_element_type.37
  1.8 0.8 convert_element_type.38.a_ref
  2.6 14.4 %deposit.1 = f32[4,8,128,128]{3,2,1,0:T(8,128)} custom-call(s32[3]{0:T(128)} %shift_ref.3, s32[640,128]{1,0:T(8,128)} %bitcast.171, f32[3,81920]{1,0:T(4,128)} %v_ref.3), custom_call_target="tpu_custom_call" | custom-call | tf_op jit(solution)/shard_map/deposit/pallas_call | solution.py:347
  17.0 21.2 %halo.1 = (f32[2,2,6,128,128]{4,3,2,1,0:T(8,128)}, f32[3,128,128]{2,1,0:T(8,128)}) custom-call(f32[4,2,2,2,128,128]{5,4,3,2,1,0:T(8,128)} %bitcast.167, f32[128,128]{1,0:T(8,128)} %convert_element_type.38.a_ref), custom_call_target="tpu_custom_call" | custom-call | tf_op jit(solution)/shard_map/halo/pallas_call | solution.py:363
  38.2 1.0 all_to_all.35
  39.2 0.8 copy.35
  40.1 4.5 %all-to-all-start = ((f32[3,4,4096]{2,0,1:T(4,128)}), f32[3,4,4096]{2,0,1:T(4,128)S(1)}, u32[]{:S(2)}, u32[]{:S(2)}) async-start(f32[3,4,4096]{2,0,1:T(4,128)} %copy.35), calls=%async_computation | async-start | bytes 524288 | tf_op jit(solution)/shard_map/all_to_all | solution.py:444
  44.8 6.9 %all-to-all-done = f32[3,4,4096]{2,0,1:T(4,128)S(1)} async-done(((f32[3,4,4096]{2,0,1:T(4,128)}), f32[3,4,4096]{2,0,1:T(4,128)S(1)}, u32[]{:S(2)}, u32[]{:S(2)}) %all-to-all-start) | async-done | bytes 196640 | tf_op jit(solution)/shard_map/all_to_all | solution.py:444
  52.2 2.1 %fusion.10 = f32[64,1,3,8,32]{0,4,3,2,1:T(8,128)S(1)} fusion(f32[4,3,8,32,16]{4,3,2,1,0:T(8,128)S(1)} %reshape.221, s32[4,16]{1,0:T(4,128)S(1)} %iota_add_fusion.1), kind=kOutput, calls=%fused_computation.19 | convolution fusion | flops 37855232 | bytes 393472 | tf_op jit(solution)/shard_map/gcyxz,gzk->kcyx/dot_general | solution.py:452
  54.2 2.1 %convolution_bitcast_fusion.2 = f32[64,1,3,8,32]{0,4,3,2,1:T(8,128)S(1)} fusion(f32[4,3,8,32,16]{4,3,2,1,0:T(8,128)S(1)} %reshape.221, s32[4,16]{1,0:T(4,128)S(1)} %iota_add_fusion.1), kind=kOutput, calls=%fused_computation.9 | convolution fusion | flops 37806080 | bytes 393472 | tf_op jit(solution)/shard_map/gcyxz,gzk->kcyx/dot_general | solution.py:451
  56.4 1.1 copy.39
  57.5 3.7 %all-to-all-start.1 = ((f32[64,6,256]{2,1,0:T(8,128)}), f32[64,6,256]{2,1,0:T(8,128)S(1)}, u32[]{:S(2)}, u32[]{:S(2)}) async-start(f32[64,6,256]{2,1,0:T(8,128)} %copy.39), calls=%async_computation.1 | async-start | bytes 1048576 | tf_op jit(solution)/shard_map/all_to_all | solution.py:454
  61.2 11.2 %collide.1 = f32[3,81920]{1,0:T(4,128)} custom-call(s32[3]{0:T(128)} %shift_ref.3, s32[640,128]{1,0:T(8,128)} %bitcast.172, f32[3,81920]{1,0:T(4,128)} %v_ref.3, f32[2,2,6,128,128]{4,3,2,1,0:T(8,128)} %get-tuple-element.38.tab_ref), custom_call_target="tpu_custom_call" | custom-call | flops 14745600 | bytes 4000000 | tf_op jit(solution)/shard_map/collide/pallas_call | solution.py:400
  72.7 3.1 %all-to-all-done.1 = f32[64,6,256]{2,1,0:T(8,128)S(1)} async-done(((f32[64,6,256]{2,1,0:T(8,128)}), f32[64,6,256]{2,1,0:T(8,128)S(1)}, u32[]{:S(2)}, u32[]{:S(2)}) %all-to-all-start.1) | async-done | bytes 393248 | tf_op jit(solution)/shard_map/all_to_all | solution.py:454
  76.3 1.4 convolution_bitcast_fusion.4
  77.7 1.4 convolution_bitcast_fusion.6
  79.1 1.4 fusion.6
  80.6 1.4 fusion.8
  82.1 2.3 %copy.44 = f32[64,8,2,3,32]{4,3,2,1,0:T(4,128)S(1)} copy(f32[64,8,2,3,32]{0,4,3,1,2:T(8,128)S(1)} %pad_maximum_fusion.1) | data formatting | bytes 786432 | tf_op jit(solution)/shard_map/stack | solution.py:472
  84.4 2.0 %all_to_all.41 = f32[4,16,1536]{2,1,0:T(8,128)} reshape(f32[64,8,2,3,32]{4,3,2,1,0:T(4,128)S(1)} %copy.44) | data formatting | bytes 786432 | tf_op jit(solution)/shard_map/all_to_all | solution.py:473
  86.4 3.8 %all-to-all-start.2 = ((f32[4,16,1536]{2,1,0:T(8,128)}), f32[4,16,1536]{2,1,0:T(8,128)S(1)}, u32[]{:S(2)}, u32[]{:S(2)}) async-start(f32[4,16,1536]{2,1,0:T(8,128)} %all_to_all.41), calls=%async_computation.2 | async-start | bytes 786432 | tf_op jit(solution)/shard_map/all_to_all | solution.py:473
  90.2 7.6 %all-to-all-done.2 = f32[4,16,1536]{2,1,0:T(8,128)S(1)} async-done(((f32[4,16,1536]{2,1,0:T(8,128)}), f32[4,16,1536]{2,1,0:T(8,128)S(1)}, u32[]{:S(2)}, u32[]{:S(2)}) %all-to-all-start.2) | async-done | bytes 393248 | tf_op jit(solution)/shard_map/all_to_all | solution.py:473
  97.9 1.3 reshape.202
  99.2 0.6 fusion.102
  99.8 1.6 %convolution_bitcast_fusion.8 = f32[128,16,8,3]{0,1,3,2:T(8,128)S(1)} fusion(f32[16,4,8,1,3,32]{5,4,3,2,0,1:T(4,128)S(1)} %get-tuple-element.79, s32[4,32]{1,0:T(4,128)S(1)} %iota_add_fusion.2), kind=kOutput, calls=%fused_computation.23 | convolution fusion | flops 75726848 | bytes 393728 | tf_op jit(solution)/shard_map/ygzcx,gxk->czyk/dot_general | solution.py:486
  101.4 1.6 %convolution_bitcast_fusion.10 = f32[128,16,8,3]{0,1,3,2:T(8,128)S(1)} fusion(f32[16,4,8,1,3,32]{5,4,3,2,0,1:T(4,128)S(1)} %get-tuple-element.78, s32[4,32]{1,0:T(4,128)S(1)} %iota_add_fusion.2), kind=kOutput, calls=%fused_computation.27 | convolution fusion | flops 75726848 | bytes 393728 | tf_op jit(solution)/shard_map/ygzcx,gxk->czyk/dot_general | solution.py:483
  103.0 1.7 %fusion.12 = f32[1,3,8,16,128]{4,3,1,2,0:T(8,128)S(1)} fusion(f32[128,16,8,3]{0,1,3,2:T(8,128)S(1)} %convolution_bitcast_fusion.8, f32[16,4,8,1,3,32]{5,4,3,2,0,1:T(4,128)S(1)} %get-tuple-element.78, s32[4,32]{1,0:T(4,128)S(1)} %iota_add_fusion.2), kind=kOutput, calls=%fused_computation.22 | convolution fusion | flops 75776000 | bytes 590336 | tf_op jit(solution)/shard_map/ygzcx,gxk->czyk/dot_general | solution.py:486
  104.7 1.7 %fusion.14 = f32[1,3,8,16,128]{4,3,1,2,0:T(8,128)S(1)} fusion(f32[128,16,8,3]{0,1,3,2:T(8,128)S(1)} %convolution_bitcast_fusion.10, f32[16,4,8,1,3,32]{5,4,3,2,0,1:T(4,128)S(1)} %get-tuple-element.79, s32[4,32]{1,0:T(4,128)S(1)} %iota_add_fusion.2), kind=kOutput, calls=%fused_computation.26 | convolution fusion | flops 75776000 | bytes 590336 | tf_op jit(solution)/shard_map/ygzcx,gxk->czyk/dot_general | solution.py:483
  106.4 3.9 %while.13 = (s32[]{:T(128)}, f32[8,32]{1,0:T(8,128)S(1)}, f32[8,32]{1,0:T(8,128)S(1)}, f32[8,16,128]{2,1,0:T(8,128)S(1)}, s32[8,16,128]{2,1,0:T(8,128)S(1)}, /*index=5*/s32[]{:T(128)}, s32[]{:T(128)}) while((s32[]{:T(128)}, f32[8,32]{1,0:T(8,128)S(1)}, f32[8,32]{1,0:T(8,128)S(1)}, f32[8,16,128]{2,1,0:T(8,128)S(1)}, ...), condition=%wide.region_3.4_spmd.clone, body=%wide.region_1.3_spmd.clone.sunk | while | flops 1048546 | bytes 58213 | solution.py:510
  110.3 0.8 copy.47
  111.1 37.5 %all-reduce = (f32[32]{0:T(128)S(1)}, f32[32]{0:T(128)S(1)}) all-reduce(f32[32]{0:T(128)S(1)} %reduce_sum.37, f32[32]{0:T(128)S(1)} %reduce_sum.38), channel_id=1, replica_groups=mesh['gx'=4,'gy'=2,'gz'=4] {'gx','gy','gz'}, use_global_device_ids=true, to_apply=%region_5.6 | all-reduce | flops 64 | bytes 512 | tf_op jit(solution)/shard_map/psum | solution.py:511
  148.6 0.5 div.3
  (72 shorter events, 5.5 us)
Async XLA Ops:
  40.1 11.6 %all-to-all-start = ((f32[3,4,4096]{2,0,1:T(4,128)}), f32[3,4,4096]{2,0,1:T(4,128)S(1)}, u32[]{:S(2)}, u32[]{:S(2)}) async-start(f32[3,4,4096]{2,0,1:T(4,128)} %copy.35), calls=%async_computation | async-start | bytes 524288 | tf_op jit(solution)/shard_map/all_to_all | solution.py:444
  57.5 18.2 %all-to-all-start.1 = ((f32[64,6,256]{2,1,0:T(8,128)}), f32[64,6,256]{2,1,0:T(8,128)S(1)}, u32[]{:S(2)}, u32[]{:S(2)}) async-start(f32[64,6,256]{2,1,0:T(8,128)} %copy.39), calls=%async_computation.1 | async-start | bytes 1048576 | tf_op jit(solution)/shard_map/all_to_all | solution.py:454
  86.4 11.5 %all-to-all-start.2 = ((f32[4,16,1536]{2,1,0:T(8,128)}), f32[4,16,1536]{2,1,0:T(8,128)S(1)}, u32[]{:S(2)}, u32[]{:S(2)}) async-start(f32[4,16,1536]{2,1,0:T(8,128)} %all_to_all.41), calls=%async_computation.2 | async-start | bytes 786432 | tf_op jit(solution)/shard_map/all_to_all | solution.py:473
where the time goes:
time: 151 us; the launch traced here: 149 us
  Pallas kernels  46.8 us (31%)
  blocking collectives  37.5 us (25%)
  matrix products  17.9 us (12%)
  waiting for transfers between devices  17.6 us (12%)
  local copies, waits for them, and re-layouts  13 us (9%)
  starting transfers between devices  11.9 us (8%)
  other arithmetic  3.34 us (2%)
    psum x1, blocking collectives, per_device(): lax.psum((jnp.sum(plane_sums, axis=0), jnp.sum(plane_counts, axis=0)), ('...  37.5 us
    pallas_call x1, Pallas kernels, halo(): pl.pallas_call(halo_kernel, in_specs=[pl.BlockSpec(memory_space=VMEM)] *...  21.2 us
    pallas_call x1, Pallas kernels, deposit(): pl.pallas_call(deposit_kernel, grid=(tiles // 8,), in_specs=[pl.BlockSpec...  14.4 us
    pallas_call x1, Pallas kernels, collide_particles(): pl.pallas_call(collide_kernel, grid=(tiles // 8,), in_specs=[pl.BlockSpec...  11.2 us
    all_to_all x1, waiting for transfers between devices, per_device(): lax.all_to_all(stacked_y, 'gx', split_axis=0, concat_axis=1, tiled=True)  7.63 us
    all_to_all x1, waiting for transfers between devices, per_device(): lax.all_to_all(cell_velocity, 'gz', split_axis=1, concat_axis=0, tiled=True)  6.9 us
    all_to_all x1, starting transfers between devices, per_device(): lax.all_to_all(cell_velocity, 'gz', split_axis=1, concat_axis=0, tiled=True)  4.52 us
    all_to_all x1, starting transfers between devices, per_device(): lax.all_to_all(stacked_y, 'gx', split_axis=0, concat_axis=1, tiled=True)  3.75 us
  transfers between devices with their start and end apart: 3, of which 3 were waited for; matrix products, arithmetic and copies ran while one was open for 0% of the time, Pallas kernels for 8%

commit v1 on v0

--- a/solution.py
+++ b/solution.py
@@ -3,6 +3,7 @@
 
 import jax
 import jax.numpy as jnp
+import numpy as np
 from jax import lax
 from jax.experimental import pallas as pl
 from jax.experimental.pallas import tpu as pltpu
@@ -15,7 +16,7 @@
 
 ROT_COS = math.cos(130.0 * math.pi / 180.0)
 ROT_SIN = math.sin(130.0 * math.pi / 180.0)
-HIGH = lax.Precision.HIGHEST
+HIGH = lax.Precision.HIGH
 F32 = jnp.float32
 VMEM = pltpu.VMEM
 
@@ -413,15 +414,100 @@
     )(grid_shift, place, velocity, tables)
 
 
+def shell_kernel(lengths, shells, m_ref, out_ref, bins, mine, others, send_sem, recv_sem):
+    names = ("gx", "gy", "gz")
+    sizes = [lax.axis_size(name) for name in names]
+    at = [lax.axis_index(name) for name in names]
+    peers = []
+    for dx in range(sizes[0]):
+        for dy in range(sizes[1]):
+            for dz in range(sizes[2]):
+                if dx or dy or dz:
+                    peers.append(
+                        tuple(lax.rem(at[d] + step, sizes[d]) for d, step in enumerate((dx, dy, dz)))
+                    )
+    barrier = pltpu.get_barrier_semaphore()
+    for peer in peers:
+        pl.semaphore_signal(
+            barrier, inc=1, device_id=peer, device_id_type=pl.DeviceIdType.MESH
+        )
+    length_x, length_y, length_z = lengths
+    rows = m_ref.shape[2]
+    depth_y = length_y // sizes[0]
+    depth_z = length_z // (sizes[1] * sizes[2])
+    energy = jnp.zeros((rows, length_x), F32)
+    for part in range(2):
+        for c in range(3):
+            value = m_ref[part, c]
+            energy = energy + value * value
+    row = iota((rows, length_x), 0)
+    kz = (at[1] * sizes[2] + at[2]) * depth_z + lax.div(row, depth_y)
+    ky = at[0] * depth_y + lax.rem(row, depth_y)
+    kx = iota((rows, length_x), 1)
+    square = jnp.zeros((rows, length_x), jnp.int32)
+    for wave, length in ((kx, length_x), (ky, length_y), (kz, length_z)):
+        signed = jnp.where(wave >= length // 2, wave - length, wave)
+        square = square + signed * signed
+    shell = jnp.floor(jnp.sqrt(square.astype(F32))).astype(jnp.int32)
+    shell = jnp.where((shell + 1) * (shell + 1) <= square, shell + 1, shell)
+    shell = jnp.where(shell * shell > square, shell - 1, shell)
+    for s in range(shells):
+        member = shell == s
+        bins[0, s : s + 1, :] = jnp.sum(jnp.where(member, energy, 0.0), axis=0, keepdims=True)
+        bins[1, s : s + 1, :] = jnp.sum(jnp.where(member, 1.0, 0.0), axis=0, keepdims=True)
+    width = bins.shape[2]
+    diagonal = iota((shells, width), 0) == iota((shells, width), 1)
+    sub = iota((8, width), 0)
+    packed = jnp.zeros((8, width), F32)
+    for f in range(2):
+        column = jnp.sum(bins[f], axis=1, keepdims=True)
+        line = jnp.sum(jnp.where(diagonal, column, 0.0), axis=0, keepdims=True)
+        packed = jnp.where(sub == f, jnp.broadcast_to(line, (8, width)), packed)
+    mine[...] = packed
+    pl.semaphore_wait(barrier, len(peers))
+    copies = [
+        pltpu.make_async_remote_copy(
+            src_ref=mine, dst_ref=others.at[slot], send_sem=send_sem.at[slot],
+            recv_sem=recv_sem.at[slot], device_id=peer, device_id_type=pl.DeviceIdType.MESH,
+        )
+        for slot, peer in enumerate(peers)
+    ]
+    for copy in copies:
+        copy.start()
+    for copy in copies:
+        copy.wait()
+    total = packed + jnp.sum(others[...], axis=0)
+    out_ref[...] = total / jnp.maximum(roll(total, -1, 0), 1.0)
+
+
+def shell_spectrum(modes, lengths):
+    shells = min(lengths) // 2
+    width = lengths[0]
+    count = lax.axis_size("gx") * lax.axis_size("gy") * lax.axis_size("gz")
+    dma = pltpu.SemaphoreType.DMA
+    rows = modes.reshape(2, 3, -1, width)
+    out = pl.pallas_call(
+        functools.partial(shell_kernel, lengths, shells),
+        in_specs=[pl.BlockSpec(memory_space=VMEM)],
+        out_specs=pl.BlockSpec(memory_space=VMEM),
+        out_shape=jax.ShapeDtypeStruct((8, width), F32),
+        scratch_shapes=[
+            VMEM((2, shells, width), F32),
+            VMEM((8, width), F32),
+            VMEM((count - 1, 8, width), F32),
+            dma((count - 1,)),
+            dma((count - 1,)),
+        ],
+        compiler_params=pltpu.CompilerParams(collective_id=1, has_side_effects=True),
+        name="shells",
+    )(rows)
+    return out[0, :shells]
+
+
 def phase_tables(positions, length):
-    phase_step = positions[..., None] * jnp.arange(length, dtype=jnp.int32) % length
-    angle = phase_step.astype(jnp.float32) * (2.0 * math.pi / length)
-    return (jnp.cos(angle), jnp.sin(angle))
-
-
-def signed_wave(first_wave, count_here, length):
-    wave = first_wave + jnp.arange(count_here, dtype=jnp.int32)
-    return jnp.where(wave >= length // 2, wave - length, wave)
+    steps = positions[..., None] * np.arange(length) % length
+    angle = steps * (2.0 * math.pi / length)
+    return np.cos(angle).astype(np.float32), np.sin(angle).astype(np.float32)
 
 
 def per_device(velocity, particle_place, grid_shift, rotation_axis):
@@ -443,75 +529,26 @@
     length_z = size_z * count_z
     arrived = lax.all_to_all(cell_velocity, "gz", split_axis=1, concat_axis=0, tiled=True)
     arrived = arrived.reshape(count_z, 3, rows_y, size_x, size_z)
-    position_z = (
-        jnp.arange(count_z, dtype=jnp.int32)[:, None] * size_z
-        + jnp.arange(size_z, dtype=jnp.int32)[None, :]
-    )
-    cos_z, sin_z = phase_tables(position_z, length_z)
-    real_z = jnp.einsum("gcyxz,gzk->kcyx", arrived, cos_z, precision=HIGH)
-    imag_z = -jnp.einsum("gcyxz,gzk->kcyx", arrived, sin_z, precision=HIGH)
-    stacked_z = jnp.stack([real_z, imag_z], axis=1).reshape(length_z, 6, rows_y * size_x)
+    cos_z, sin_z = phase_tables(np.arange(length_z).reshape(count_z, size_z), length_z)
+    both_z = np.stack([cos_z, -sin_z], axis=-1)
+    stacked_z = jnp.einsum("gcyxz,gzkp->kpcyx", arrived, both_z, precision=HIGH)
+    stacked_z = stacked_z.reshape(length_z, 6, rows_y * size_x)
     pencil = lax.all_to_all(stacked_z, ("gy", "gz"), split_axis=0, concat_axis=1, tiled=True)
-    outer_count, outer_step, inner_count, inner_step = (count_y, size_y, count_z, rows_y)
     depth_z = length_z // (count_y * count_z)
-    pencil = pencil.reshape(depth_z, outer_count, inner_count, 2, 3, rows_y, size_x)
-    position_y = (
-        jnp.arange(outer_count, dtype=jnp.int32)[:, None, None] * outer_step
-        + jnp.arange(inner_count, dtype=jnp.int32)[None, :, None] * inner_step
-        + jnp.arange(rows_y, dtype=jnp.int32)[None, None, :]
-    )
-    cos_y, sin_y = phase_tables(position_y, length_y)
-    part_re = pencil[:, :, :, 0]
-    part_im = pencil[:, :, :, 1]
-    real_y = jnp.einsum("zabcyx,abyk->kzcx", part_re, cos_y, precision=HIGH) + jnp.einsum(
-        "zabcyx,abyk->kzcx", part_im, sin_y, precision=HIGH
-    )
-    imag_y = jnp.einsum("zabcyx,abyk->kzcx", part_im, cos_y, precision=HIGH) - jnp.einsum(
-        "zabcyx,abyk->kzcx", part_re, sin_y, precision=HIGH
-    )
-    stacked_y = jnp.stack([real_y, imag_y], axis=2).reshape(length_y, depth_z * 6 * size_x)
+    pencil = pencil.reshape(depth_z, count_y, count_z, 2, 3, rows_y, size_x)
+    cos_y, sin_y = phase_tables(np.arange(length_y).reshape(count_y, count_z, rows_y), length_y)
+    both_y = np.stack([np.stack([cos_y, -sin_y]), np.stack([sin_y, cos_y])])
+    stacked_y = jnp.einsum("zabpcyx,pqabyk->kzqcx", pencil, both_y, precision=HIGH)
+    stacked_y = stacked_y.reshape(length_y, depth_z * 6 * size_x)
     columns = lax.all_to_all(stacked_y, "gx", split_axis=0, concat_axis=1, tiled=True)
     depth_y = length_y // count_x
     columns = columns.reshape(depth_y, count_x, depth_z, 2, 3, size_x)
-    position_x = (
-        jnp.arange(count_x, dtype=jnp.int32)[:, None] * size_x
-        + jnp.arange(size_x, dtype=jnp.int32)[None, :]
-    )
-    cos_x, sin_x = phase_tables(position_x, length_x)
-    col_re = columns[:, :, :, 0]
-    col_im = columns[:, :, :, 1]
-    real_x = jnp.einsum("ygzcx,gxk->czyk", col_re, cos_x, precision=HIGH) + jnp.einsum(
-        "ygzcx,gxk->czyk", col_im, sin_x, precision=HIGH
-    )
-    imag_x = jnp.einsum("ygzcx,gxk->czyk", col_im, cos_x, precision=HIGH) - jnp.einsum(
-        "ygzcx,gxk->czyk", col_re, sin_x, precision=HIGH
-    )
+    cos_x, sin_x = phase_tables(np.arange(length_x).reshape(count_x, size_x), length_x)
     norm_scale = 1.0 / math.sqrt(length_x * length_y * length_z)
-    modes = jnp.stack([real_x, imag_x], axis=0) * norm_scale
-    energy = jnp.sum(modes * modes, axis=(0, 1))
-    first_z = (lax.axis_index("gy") * count_z + lax.axis_index("gz")) * depth_z
-    first_y = lax.axis_index("gx") * depth_y
-    wave_z = signed_wave(first_z, depth_z, length_z)
-    wave_y = signed_wave(first_y, depth_y, length_y)
-    wave_x = signed_wave(0, length_x, length_x)
-    square = wave_z[:, None, None] ** 2 + wave_y[None, :, None] ** 2 + wave_x[None, None, :] ** 2
-    shell_index = jnp.floor(jnp.sqrt(square.astype(jnp.float32))).astype(jnp.int32)
-    shells = min(min(length_x, length_y), length_z) // 2
-    ladder = jnp.arange(shells, dtype=jnp.int32)
-
-    def bin_plane(plane_pair):
-        plane_energy, plane_shell = plane_pair
-        member_shell = (plane_shell[..., None] == ladder).astype(jnp.float32)
-        return (
-            jnp.einsum("yx,yxs->s", plane_energy, member_shell, precision=HIGH),
-            jnp.sum(member_shell, axis=(0, 1)),
-        )
-
-    plane_sums, plane_counts = lax.map(bin_plane, (energy, shell_index))
-    shell_totals = lax.psum(
-        (jnp.sum(plane_sums, axis=0), jnp.sum(plane_counts, axis=0)), ("gx", "gy", "gz")
-    )
-    spectrum = shell_totals[0] / shell_totals[1]
+    both_x = np.stack([np.stack([cos_x, -sin_x]), np.stack([sin_x, cos_x])])
+    both_x = (both_x * norm_scale).astype(np.float32)
+    modes = jnp.einsum("ygzpcx,pqgxk->qczyk", columns, both_x, precision=HIGH)
+    spectrum = shell_spectrum(modes, (length_x, length_y, length_z))
     return (new_velocity, modes, spectrum)
 
 

time: 151 us -> 109 us (0.72)
  waiting for transfers between devices: 17.6 us -> 0.01 us
  matrix products: 17.9 us -> 3.44 us
  Pallas kernels: 46.8 us -> 58.1 us
  starting transfers between devices: 11.9 us -> 3.46 us
  blocking collectives: 37.5 us -> 29.5 us
  other arithmetic: 3.34 us -> 0.97 us
  local copies, waits for them, and re-layouts: 13 us -> 11.1 us
    psum x1 -> x0, blocking collectives: 37.5 us -> none  [per_device(): lax.psum((jnp.sum(plane_sums, axis=0), jnp.sum(plane_counts, axis=0)), ('...]
    all_to_all x0 -> x2, blocking collectives: none -> 29.5 us  [the longest x1 17.5 us: per_device(): lax.all_to_all(stacked_z, ('gy', 'gz'), split_axis=0, concat_axis=1, tile...]
    dot_general x18 -> x3, matrix products: 17.9 us -> 3.44 us  [the longest x1 1.42 us: per_device(): jnp.einsum('zabpcyx,pqabyk->kzqcx', pencil, both_y, precision=HIGH)]
    pallas_call x0 -> x1, Pallas kernels: none -> 11.3 us  [shell_spectrum(): pl.pallas_call(functools.partial(shell_kernel, lengths, shells), in_specs...]
    all_to_all x2 -> x0, waiting for transfers between devices: 9.96 us -> none  [the longest x1 6.9 us: per_device(): lax.all_to_all(cell_velocity, 'gz', split_axis=1, concat_axis=0, tiled=True)]
    all_to_all x2 -> x0, starting transfers between devices: 8.19 us -> none  [the longest x1 4.52 us: per_device(): lax.all_to_all(cell_velocity, 'gz', split_axis=1, concat_axis=0, tiled=True)]
    all_to_all x1, waiting for transfers between devices: 7.63 us -> 0.01 us  [per_device(): lax.all_to_all(stacked_y, 'gx', split_axis=0, concat_axis=1, tiled=True)]
    another operation x1 -> x0, local copies, waits for them, and re-layouts: 2.34 us -> none  [per_device(): jnp.stack([real_y, imag_y], axis=2).reshape(length_y, depth_z * 6 * size_x)]
  transfers between devices with their start and end apart: 3 -> 1, of which waited for: 3 -> 0; matrix products, arithmetic and copies ran while one was open for 0% -> 0% of each run, Pallas kernels for 8% -> 10%
where the time goes in v1:
time: 109 us; the launch traced here: 107 us
  Pallas kernels  58.1 us (53%)
  blocking collectives  29.5 us (27%)
  local copies, waits for them, and re-layouts  11.1 us (10%)
  starting transfers between devices  3.46 us (3%)
  matrix products  3.44 us (3%)
    pallas_call x1, Pallas kernels, halo(): pl.pallas_call(halo_kernel, in_specs=[pl.BlockSpec(memory_space=VMEM)] *...  21.2 us
    all_to_all x1, blocking collectives, per_device(): lax.all_to_all(stacked_z, ('gy', 'gz'), split_axis=0, concat_axis=1, tile...  17.5 us
    pallas_call x1, Pallas kernels, deposit(): pl.pallas_call(deposit_kernel, grid=(tiles // 8,), in_specs=[pl.BlockSpec...  14.4 us
    all_to_all x1, blocking collectives, per_device(): lax.all_to_all(cell_velocity, 'gz', split_axis=1, concat_axis=0, tiled=True)  12 us
    pallas_call x1, Pallas kernels, shell_spectrum(): pl.pallas_call(functools.partial(shell_kernel, lengths, shells), in_specs...  11.3 us
    pallas_call x1, Pallas kernels, collide_particles(): pl.pallas_call(collide_kernel, grid=(tiles // 8,), in_specs=[pl.BlockSpec...  11.2 us
    all_to_all x1, starting transfers between devices, per_device(): lax.all_to_all(stacked_y, 'gx', split_axis=0, concat_axis=1, tiled=True)  3.46 us
    transpose x1, local copies, waits for them, and re-layouts, per_device(): jnp.einsum('zabpcyx,pqabyk->kzqcx', pencil, both_y, precision=HIGH)  2.34 us
  transfers between devices with their start and end apart: 1, of which 0 were waited for; matrix products, arithmetic and copies ran while one was open for 0% of the time, Pallas kernels for 10%

profile of v1, /device:TPU:0, one launch (start us, length us, event | category | flops | bytes accessed | tf_op | source)
XLA Modules:
  0.0 107.5 jit_solution(15402551616104606844)
XLA Ops:
  0.6 1.0 convert_element_type.5
  1.6 0.2 copy.22
  1.8 0.8 convert_element_type.6.a_ref
  2.6 14.4 %deposit.1 = f32[4,8,128,128]{3,2,1,0:T(8,128)} custom-call(s32[3]{0:T(128)} %shift_ref.3, s32[640,128]{1,0:T(8,128)} %bitcast.58, f32[3,81920]{1,0:T(4,128)} %v_ref.3), custom_call_target="tpu_custom_call" | custom-call | tf_op jit(solution)/shard_map/deposit/pallas_call | solution.py:348
  17.1 21.2 %halo.1 = (f32[2,2,6,128,128]{4,3,2,1,0:T(8,128)}, f32[3,128,128]{2,1,0:T(8,128)}) custom-call(f32[4,2,2,2,128,128]{5,4,3,2,1,0:T(8,128)} %bitcast.52, f32[128,128]{1,0:T(8,128)} %convert_element_type.6.a_ref), custom_call_target="tpu_custom_call" | custom-call | tf_op jit(solution)/shard_map/halo/pallas_call | solution.py:364
  38.3 0.0 copy-start.2
  38.3 1.0 all_to_all.35
  39.3 0.1 copy.23
  39.5 12.0 %all_to_all.47 = f32[3,4,4096]{2,0,1:T(4,128)S(1)} all-to-all(f32[3,4,4096]{2,0,1:T(4,128)S(1)} %copy.23), channel_id=1, replica_groups=mesh['gx'=4,'gy'=2,'gz'=4] {'gz'}, dimensions={1} | all-to-all | bytes 393216 | tf_op jit(solution)/shard_map/all_to_all | solution.py:530
  51.5 0.5 reshape.58
  52.0 0.0 copy-done.2
  52.0 1.1 %fusion.4 = f32[64,2,3,8,32,1]{0,4,3,2,5,1:T(8,128)S(1)} fusion(f32[4,3,8,32,16]{4,3,2,1,0:T(8,128)S(1)} %reshape.58, f32[4,16,64,2,1,1]{2,1,0,5,4,3:T(8,128)S(1)} %copy-done.2), kind=kOutput, calls=%fused_computation.4 | convolution fusion | flops 37748736 | bytes 622592 | tf_op jit(solution)/shard_map/gcyxz,gzkp->kpcyx/dot_general | solution.py:534
  53.1 0.4 copy.26
  53.5 0.0 copy-start.1
  53.5 17.5 %all_to_all.48 = f32[64,6,256]{2,1,0:T(8,128)S(1)} all-to-all(f32[64,6,256]{2,1,0:T(8,128)S(1)} %copy.26), channel_id=1, replica_groups=mesh['gx'=4,'gy'=2,'gz'=4] {'gy','gz'}, dimensions={0} | all-to-all | bytes 786432 | tf_op jit(solution)/shard_map/all_to_all | solution.py:536
  71.0 0.4 reshape.59
  71.4 0.0 copy-done.1
  71.4 1.4 %fusion.6 = f32[64,8,2,3,32]{0,4,3,1,2:T(8,128)S(1)} fusion(f32[2,2,2,4,8,64,1,1]{5,4,3,2,7,6,1,0:T(8,128)S(1)} %copy-done.1, f32[8,2,4,2,3,8,32]{6,5,4,3,0,2,1:T(8,128)S(1)} %reshape.59), kind=kOutput, calls=%fused_computation.6 | convolution fusion | flops 75497472 | bytes 851968 | tf_op jit(solution)/shard_map/zabpcyx,pqabyk->kzqcx/dot_general | solution.py:541
  72.9 2.3 %copy.30 = f32[64,8,2,3,32]{4,3,2,1,0:T(4,128)S(1)} copy(f32[64,8,2,3,32]{0,4,3,1,2:T(8,128)S(1)} %fusion.6) | data formatting | bytes 786432 | tf_op jit(solution)/shard_map/zabpcyx,pqabyk->kzqcx/transpose | solution.py:541
  75.2 2.0 %all_to_all.41 = f32[4,16,1536]{2,1,0:T(8,128)} reshape(f32[64,8,2,3,32]{4,3,2,1,0:T(4,128)S(1)} %copy.30) | data formatting | bytes 786432 | tf_op jit(solution)/shard_map/all_to_all | solution.py:543
  77.2 3.5 %all-to-all-start.2 = ((f32[4,16,1536]{2,1,0:T(8,128)}), f32[4,16,1536]{2,1,0:T(8,128)S(1)}, u32[]{:S(2)}, u32[]{:S(2)}) async-start(f32[4,16,1536]{2,1,0:T(8,128)} %all_to_all.41), calls=%async_computation.2 | async-start | bytes 786432 | tf_op jit(solution)/shard_map/all_to_all | solution.py:543
  80.6 11.2 %collide.1 = f32[3,81920]{1,0:T(4,128)} custom-call(s32[3]{0:T(128)} %shift_ref.3, s32[640,128]{1,0:T(8,128)} %bitcast.59, f32[3,81920]{1,0:T(4,128)} %v_ref.3, f32[2,2,6,128,128]{4,3,2,1,0:T(8,128)} %get-tuple-element.5.tab_ref), custom_call_target="tpu_custom_call" | custom-call | flops 14745600 | bytes 4000000 | tf_op jit(solution)/shard_map/collide/pallas_call | solution.py:401
  91.9 0.0 copy-start
  91.9 0.0 all-to-all-done.2
  91.9 1.3 %reshape.47 = f32[16,4,8,2,3,32]{5,4,3,2,0,1:T(4,128)S(1)} reshape(f32[16,4,1536]{2,0,1:T(8,128)S(1)} %bitcast.56) | data formatting | bytes 786432 | tf_op jit(solution)/shard_map/reshape | solution.py:545
  93.2 0.0 copy-done
  93.2 0.9 fusion.9
  94.1 0.9 copy.33
  95.0 11.3 %shells.1 = f32[8,128]{1,0:T(8,128)} custom-call(f32[2,3,128,128]{3,2,1,0:T(8,128)} %bitcast.57), custom_call_target="tpu_custom_call" | custom-call | tf_op jit(solution)/shard_map/shells/pallas_call | solution.py:489
  106.3 1.2 %slice_bitcast_fusion = f32[32]{0:T(128)} fusion(f32[8,128]{1,0:T(8,128)} %shells.1), kind=kLoop, calls=%fused_computation.9 | loop fusion | bytes 256 | tf_op jit(solution)/shard_map/squeeze | solution.py:504
Async XLA Ops:
  38.3 13.7 %copy-start.2 = (f32[4,16,64,2,1,1]{2,1,0,5,4,3:T(8,128)S(1)}, f32[4,16,64,2,1,1]{2,1,0,5,4,3:T(8,128)}, u32[]{:S(2)}) copy-start(f32[4,16,64,2,1,1]{2,1,0,5,4,3:T(8,128)} %constant.9) | copy-start | bytes 98308
  53.5 17.9 %copy-start.1 = (f32[2,2,2,4,8,64,1,1]{5,4,3,2,7,6,1,0:T(8,128)S(1)}, f32[2,2,2,4,8,64,1,1]{5,4,3,2,7,6,1,0:T(8,128)}, u32[]{:S(2)}) copy-start(f32[2,2,2,4,8,64,1,1]{5,4,3,2,7,6,1,0:T(8,128)} %constant.10) | copy-start | bytes 196612
  77.2 14.7 %all-to-all-start.2 = ((f32[4,16,1536]{2,1,0:T(8,128)}), f32[4,16,1536]{2,1,0:T(8,128)S(1)}, u32[]{:S(2)}, u32[]{:S(2)}) async-start(f32[4,16,1536]{2,1,0:T(8,128)} %all_to_all.41), calls=%async_computation.2 | async-start | bytes 786432 | tf_op jit(solution)/shard_map/all_to_all | solution.py:543
  91.9 1.3 %copy-start = (f32[2,2,4,32,128,1,1]{4,3,0,2,1,6,5:T(8,128)S(1)}, f32[2,2,4,32,128,1,1]{4,3,0,2,1,6,5:T(8,128)}, u32[]{:S(2)}) copy-start(f32[2,2,4,32,128,1,1]{4,3,0,2,1,6,5:T(8,128)} %constant.11) | copy-start | bytes 786436

commit v2 on v1

--- a/solution.py
+++ b/solution.py
@@ -106,7 +106,7 @@
     s_ref, a_ref, tab_ref, cell_ref,
     y_low, y_up, ya_up, grid_sums, axis_ext, xs, face_sums,
     x_send_up, x_send_down, x_low, x_up, z_send_up, z_send_down, z_low, z_up,
-    total, work, tables, send_sem, recv_sem,
+    total, work, tables, outgoing, incoming, send_sem, recv_sem, cell_send, cell_recv,
 ):
     rows = 136
     lane = iota((8, TILE), 1)
@@ -114,12 +114,16 @@
     lane_z = lane & 15
 
     barrier = pltpu.get_barrier_semaphore()
-    for name in ("gx", "gy", "gz"):
-        for side in neighbours(name):
-            pl.semaphore_signal(
-                barrier, inc=1, device_id={name: side}, device_id_type=pl.DeviceIdType.MESH
-            )
-    pl.semaphore_wait(barrier, 6)
+    count_z = lax.axis_size("gz")
+    me_z = lax.axis_index("gz")
+    greeted = [("gx", side) for side in neighbours("gx")]
+    greeted += [("gy", side) for side in neighbours("gy")]
+    greeted += [("gz", lax.rem(me_z + step, count_z)) for step in range(1, count_z)]
+    for name, side in greeted:
+        pl.semaphore_signal(
+            barrier, inc=1, device_id={name: side}, device_id_type=pl.DeviceIdType.MESH
+        )
+    pl.semaphore_wait(barrier, len(greeted))
 
     def remote(src, dst, name, upward, slot):
         up, down = neighbours(name)
@@ -279,9 +283,7 @@
 
     xl = lane >> 4
 
-    @pl.loop(0, 16)
-    def _(k):
-        r = pl.multiple_of(k * 8, 8)
+    def cell_group(r, slot, row):
         sums = [jnp.zeros((8, TILE), F32) for _ in range(3)]
         number = jnp.zeros((8, TILE), F32)
         for bx in range(2):
@@ -306,7 +308,30 @@
                     sums = [sums[c] + drift[c] + turned[c] for c in range(3)]
         inverse = 1.0 / jnp.maximum(number, 1.0)
         for c in range(3):
-            cell_ref[c, pl.ds(r, 8), :] = sums[c] * inverse
+            outgoing[slot, c, pl.ds(row, 8), :] = sums[c] * inverse
+
+    share = outgoing.shape[2]
+    sent = []
+    for step in list(range(1, count_z)) + [0]:
+        owner = lax.rem(me_z + step, count_z)
+
+        @pl.loop(0, share // 8)
+        def _(k):
+            row = pl.multiple_of(k * 8, 8)
+            cell_group(pl.multiple_of(owner * share + row, 8), step, row)
+
+        if step:
+            copy = pltpu.make_async_remote_copy(
+                src_ref=outgoing.at[step], dst_ref=incoming.at[step - 1],
+                send_sem=cell_send.at[step - 1], recv_sem=cell_recv.at[step - 1],
+                device_id={"gz": owner}, device_id_type=pl.DeviceIdType.MESH,
+            )
+            copy.start()
+            sent.append(copy)
+    cell_ref[me_z] = outgoing[0]
+    for step in range(1, count_z):
+        sent[step - 1].wait()
+        cell_ref[lax.rem(me_z + count_z - step, count_z)] = incoming[step - 1]
 
 
 def collide_kernel(shift_ref, place_ref, v_ref, tab_ref, out_ref):
@@ -361,13 +386,15 @@
 
 def halo(sums, axis, tiles):
     dma = pltpu.SemaphoreType.DMA
+    count_z = lax.axis_size("gz")
+    share = tiles // count_z
     return pl.pallas_call(
         halo_kernel,
         in_specs=[pl.BlockSpec(memory_space=VMEM)] * 2,
         out_specs=[pl.BlockSpec(memory_space=VMEM)] * 2,
         out_shape=[
             jax.ShapeDtypeStruct((2, 2, 6, tiles, TILE), F32),
-            jax.ShapeDtypeStruct((3, tiles, TILE), F32),
+            jax.ShapeDtypeStruct((count_z, 3, share, TILE), F32),
         ],
         scratch_shapes=[
             VMEM((4, 2, 2, 8, TILE), F32),
@@ -388,8 +415,12 @@
             VMEM((2, 4, 136, TILE), F32),
             VMEM((144, TILE), F32),
             VMEM((2, 6, 136, TILE), F32),
+            VMEM((count_z, 3, share, TILE), F32),
+            VMEM((count_z - 1, 3, share, TILE), F32),
             dma((7,)),
             dma((7,)),
+            dma((count_z - 1,)),
+            dma((count_z - 1,)),
         ],
         compiler_params=pltpu.CompilerParams(collective_id=0, has_side_effects=True),
         name="halo",
@@ -414,7 +445,52 @@
     )(grid_shift, place, velocity, tables)
 
 
-def shell_kernel(lengths, shells, m_ref, out_ref, bins, mine, others, send_sem, recv_sem):
+def exchange_kernel(x_ref, out_ref, send_sem, recv_sem):
+    count_y, count_z = lax.axis_size("gy"), lax.axis_size("gz")
+    me_y, me_z = lax.axis_index("gy"), lax.axis_index("gz")
+    me = me_y * count_z + me_z
+    peers = [
+        (lax.rem(me_y + dy, count_y), lax.rem(me_z + dz, count_z))
+        for dy in range(count_y)
+        for dz in range(count_z)
+        if dy or dz
+    ]
+    barrier = pltpu.get_barrier_semaphore()
+    for y, z in peers:
+        pl.semaphore_signal(
+            barrier, inc=1, device_id={"gy": y, "gz": z}, device_id_type=pl.DeviceIdType.MESH
+        )
+    pl.semaphore_wait(barrier, len(peers))
+    copies = [
+        pltpu.make_async_remote_copy(
+            src_ref=x_ref.at[y * count_z + z], dst_ref=out_ref.at[me],
+            send_sem=send_sem.at[slot], recv_sem=recv_sem.at[slot],
+            device_id={"gy": y, "gz": z}, device_id_type=pl.DeviceIdType.MESH,
+        )
+        for slot, (y, z) in enumerate(peers)
+    ]
+    for copy in copies:
+        copy.start()
+    out_ref[me] = x_ref[me]
+    for copy in copies:
+        copy.wait()
+
+
+def exchange(blocks):
+    peers = blocks.shape[0] - 1
+    dma = pltpu.SemaphoreType.DMA
+    return pl.pallas_call(
+        exchange_kernel,
+        in_specs=[pl.BlockSpec(memory_space=VMEM)],
+        out_specs=pl.BlockSpec(memory_space=VMEM),
+        out_shape=jax.ShapeDtypeStruct(blocks.shape, F32),
+        scratch_shapes=[dma((peers,)), dma((peers,))],
+        compiler_params=pltpu.CompilerParams(collective_id=2, has_side_effects=True),
+        name="exchange",
+    )(blocks)
+
+
+def shell_kernel(lengths, shells, m_ref, n_ref, out_ref, bins, mine, others, send_sem, recv_sem):
     names = ("gx", "gy", "gz")
     sizes = [lax.axis_size(name) for name in names]
     at = [lax.axis_index(name) for name in names]
@@ -453,16 +529,12 @@
     shell = jnp.where(shell * shell > square, shell - 1, shell)
     for s in range(shells):
         member = shell == s
-        bins[0, s : s + 1, :] = jnp.sum(jnp.where(member, energy, 0.0), axis=0, keepdims=True)
-        bins[1, s : s + 1, :] = jnp.sum(jnp.where(member, 1.0, 0.0), axis=0, keepdims=True)
-    width = bins.shape[2]
+        bins[s : s + 1, :] = jnp.sum(jnp.where(member, energy, 0.0), axis=0, keepdims=True)
+    width = bins.shape[1]
     diagonal = iota((shells, width), 0) == iota((shells, width), 1)
-    sub = iota((8, width), 0)
-    packed = jnp.zeros((8, width), F32)
-    for f in range(2):
-        column = jnp.sum(bins[f], axis=1, keepdims=True)
-        line = jnp.sum(jnp.where(diagonal, column, 0.0), axis=0, keepdims=True)
-        packed = jnp.where(sub == f, jnp.broadcast_to(line, (8, width)), packed)
+    column = jnp.sum(bins[...], axis=1, keepdims=True)
+    line = jnp.sum(jnp.where(diagonal, column, 0.0), axis=0, keepdims=True)
+    packed = jnp.broadcast_to(line, (8, width))
     mine[...] = packed
     pl.semaphore_wait(barrier, len(peers))
     copies = [
@@ -477,7 +549,7 @@
     for copy in copies:
         copy.wait()
     total = packed + jnp.sum(others[...], axis=0)
-    out_ref[...] = total / jnp.maximum(roll(total, -1, 0), 1.0)
+    out_ref[...] = total / n_ref[...]
 
 
 def shell_spectrum(modes, lengths):
@@ -486,13 +558,18 @@
     count = lax.axis_size("gx") * lax.axis_size("gy") * lax.axis_size("gz")
     dma = pltpu.SemaphoreType.DMA
     rows = modes.reshape(2, 3, -1, width)
+    waves = [np.minimum(np.arange(n), n - np.arange(n)) ** 2 for n in lengths]
+    square = waves[2][:, None, None] + waves[1][None, :, None] + waves[0][None, None, :]
+    shell = np.floor(np.sqrt(square.astype(np.float64))).astype(np.int64).ravel()
+    number = np.ones((8, width), np.float32)
+    number[:, :shells] = np.bincount(shell, minlength=shells)[:shells]
     out = pl.pallas_call(
         functools.partial(shell_kernel, lengths, shells),
-        in_specs=[pl.BlockSpec(memory_space=VMEM)],
+        in_specs=[pl.BlockSpec(memory_space=VMEM)] * 2,
         out_specs=pl.BlockSpec(memory_space=VMEM),
         out_shape=jax.ShapeDtypeStruct((8, width), F32),
         scratch_shapes=[
-            VMEM((2, shells, width), F32),
+            VMEM((shells, width), F32),
             VMEM((8, width), F32),
             VMEM((count - 1, 8, width), F32),
             dma((count - 1,)),
@@ -500,7 +577,7 @@
         ],
         compiler_params=pltpu.CompilerParams(collective_id=1, has_side_effects=True),
         name="shells",
-    )(rows)
+    )(rows, jnp.asarray(number))
     return out[0, :shells]
 
 
@@ -519,7 +596,6 @@
     axis = rotation_axis.reshape(tile_count, TILE).astype(F32)
     tables, cell_sums = halo(sums.reshape(4, 2, 2, 2, tile_count, TILE), axis, tile_count)
     new_velocity = collide_particles(grid_shift, place, velocity, tables, tile_count)
-    cell_velocity = cell_sums.reshape(3, cell_count)
     count_x = lax.axis_size("gx")
     count_y = lax.axis_size("gy")
     count_z = lax.axis_size("gz")
@@ -527,18 +603,16 @@
     length_x = size_x * count_x
     length_y = size_y * count_y
     length_z = size_z * count_z
-    arrived = lax.all_to_all(cell_velocity, "gz", split_axis=1, concat_axis=0, tiled=True)
-    arrived = arrived.reshape(count_z, 3, rows_y, size_x, size_z)
+    arrived = cell_sums.reshape(count_z, 3, rows_y, size_x, size_z)
     cos_z, sin_z = phase_tables(np.arange(length_z).reshape(count_z, size_z), length_z)
     both_z = np.stack([cos_z, -sin_z], axis=-1)
     stacked_z = jnp.einsum("gcyxz,gzkp->kpcyx", arrived, both_z, precision=HIGH)
-    stacked_z = stacked_z.reshape(length_z, 6, rows_y * size_x)
-    pencil = lax.all_to_all(stacked_z, ("gy", "gz"), split_axis=0, concat_axis=1, tiled=True)
     depth_z = length_z // (count_y * count_z)
-    pencil = pencil.reshape(depth_z, count_y, count_z, 2, 3, rows_y, size_x)
+    pencil = exchange(stacked_z.reshape(count_y * count_z, -1, TILE))
+    pencil = pencil.reshape(count_y, count_z, depth_z, 2, 3, rows_y, size_x)
     cos_y, sin_y = phase_tables(np.arange(length_y).reshape(count_y, count_z, rows_y), length_y)
     both_y = np.stack([np.stack([cos_y, -sin_y]), np.stack([sin_y, cos_y])])
-    stacked_y = jnp.einsum("zabpcyx,pqabyk->kzqcx", pencil, both_y, precision=HIGH)
+    stacked_y = jnp.einsum("abzpcyx,pqabyk->kzqcx", pencil, both_y, precision=HIGH)
     stacked_y = stacked_y.reshape(length_y, depth_z * 6 * size_x)
     columns = lax.all_to_all(stacked_y, "gx", split_axis=0, concat_axis=1, tiled=True)
     depth_y = length_y // count_x

time: 109 us -> 98.4 us (0.903)
  blocking collectives: 29.5 us -> 0 us
  Pallas kernels: 58.1 us -> 75 us
  local copies, waits for them, and re-layouts: 11.1 us -> 13.3 us
    all_to_all x2 -> x0, blocking collectives: 29.5 us -> none  [the longest x1 17.5 us: per_device(): lax.all_to_all(stacked_z, ('gy', 'gz'), split_axis=0, concat_axis=1, tile...]
    pallas_call x0 -> x1, Pallas kernels: none -> 12.6 us  [exchange(): pl.pallas_call(exchange_kernel, in_specs=[pl.BlockSpec(memory_space=VMEM)...]
    pallas_call x1, Pallas kernels: 21.2 us -> 24.8 us  [halo(): pl.pallas_call(halo_kernel, in_specs=[pl.BlockSpec(memory_space=VMEM)] *...]
    reshape x3, local copies, waits for them, and re-layouts: 1.27 us -> 3.86 us  [the longest x1 1.37 us: per_device(): arrived = cell_sums.reshape(count_z, 3, rows_y, size_x, size_z)]
    all_to_all x2 -> x0, local copies, waits for them, and re-layouts: 1.16 us -> none  [per_device(): lax.all_to_all(cell_velocity, 'gz', split_axis=1, concat_axis=0, tiled=True)]
  transfers between devices with their start and end apart: 1 -> 1, of which waited for: 0 -> 0; matrix products, arithmetic and copies ran while one was open for 0% -> 0% of each run, Pallas kernels for 10% -> 12%
where the time goes in v2:
time: 98.4 us; the launch traced here: 96.9 us
  Pallas kernels  75 us (76%)
  local copies, waits for them, and re-layouts  13.3 us (14%)
  starting transfers between devices  3.46 us (4%)
  matrix products  3.44 us (3%)
    pallas_call x1, Pallas kernels, halo(): pl.pallas_call(halo_kernel, in_specs=[pl.BlockSpec(memory_space=VMEM)] *...  24.8 us
    pallas_call x1, Pallas kernels, deposit(): pl.pallas_call(deposit_kernel, grid=(tiles // 8,), in_specs=[pl.BlockSpec...  14.4 us
    pallas_call x1, Pallas kernels, exchange(): pl.pallas_call(exchange_kernel, in_specs=[pl.BlockSpec(memory_space=VMEM)...  12.6 us
    pallas_call x1, Pallas kernels, shell_spectrum(): pl.pallas_call(functools.partial(shell_kernel, lengths, shells), in_specs...  11.9 us
    pallas_call x1, Pallas kernels, collide_particles(): pl.pallas_call(collide_kernel, grid=(tiles // 8,), in_specs=[pl.BlockSpec...  11.2 us
    all_to_all x1, starting transfers between devices, per_device(): lax.all_to_all(stacked_y, 'gx', split_axis=0, concat_axis=1, tiled=True)  3.46 us
    transpose x1, local copies, waits for them, and re-layouts, per_device(): jnp.einsum('abzpcyx,pqabyk->kzqcx', pencil, both_y, precision=HIGH)  2.34 us
  transfers between devices with their start and end apart: 1, of which 0 were waited for; matrix products, arithmetic and copies ran while one was open for 0% of the time, Pallas kernels for 12%

profile of v2, /device:TPU:0, one launch (start us, length us, event | category | flops | bytes accessed | tf_op | source)
XLA Modules:
  0.0 96.9 jit_solution(4254084972158766542)
XLA Ops:
  0.6 1.0 %convert_element_type.5 = f32[32,32,16]{1,2,0:T(8,128)S(1)} convert(s32[32,32,16]{1,2,0:T(8,128)} %param.11) | non-fusion elementwise | flops 16384 | bytes 131072 | tf_op jit(solution)/shard_map/convert_element_type | solution.py:596
  1.6 0.2 copy.17
  1.8 0.8 convert_element_type.6.a_ref
  2.6 14.4 %deposit.1 = f32[4,8,128,128]{3,2,1,0:T(8,128)} custom-call(s32[3]{0:T(128)} %shift_ref.3, s32[640,128]{1,0:T(8,128)} %bitcast.53, f32[3,81920]{1,0:T(4,128)} %v_ref.3), custom_call_target="tpu_custom_call" | custom-call | tf_op jit(solution)/shard_map/deposit/pallas_call | solution.py:373
  17.1 0.0 copy-start.2
  17.1 24.8 %halo.1 = (f32[2,2,6,128,128]{4,3,2,1,0:T(8,128)}, f32[4,3,32,128]{3,2,1,0:T(8,128)}) custom-call(f32[4,2,2,2,128,128]{5,4,3,2,1,0:T(8,128)} %bitcast.49, f32[128,128]{1,0:T(8,128)} %convert_element_type.6.a_ref), custom_call_target="tpu_custom_call" | custom-call | tf_op jit(solution)/shard_map/halo/pallas_call | solution.py:391
  41.9 1.4 %reshape.37 = f32[4,3,8,32,16]{4,3,2,1,0:T(8,128)S(1)} reshape(f32[4,3,32,128]{3,2,1,0:T(8,128)} %get-tuple-element.6) | data formatting | bytes 393216 | tf_op jit(solution)/shard_map/reshape | solution.py:606
  43.3 0.0 copy-done.2
  43.3 1.1 %fusion.6 = f32[64,2,3,8,32]{0,4,3,2,1:T(8,128)S(1)} fusion(f32[4,3,8,32,16]{4,3,2,1,0:T(8,128)S(1)} %reshape.37, f32[4,16,64,2,1,1]{2,1,0,5,4,3:T(8,128)S(1)} %copy-done.2), kind=kOutput, calls=%fused_computation.6 | convolution fusion | flops 37748736 | bytes 622592 | tf_op jit(solution)/shard_map/gcyxz,gzkp->kpcyx/dot_general | solution.py:609
  44.4 0.7 copy.19
  45.1 1.1 %reshape.38.x_ref = f32[8,96,128]{2,1,0:T(8,128)} reshape(f32[64,2,3,8,32]{4,3,2,1,0:T(8,128)S(1)} %copy.19) | data formatting | bytes 786432 | tf_op jit(solution)/shard_map/reshape | solution.py:611
  46.3 0.0 copy-start.1
  46.3 12.6 %exchange.1 = f32[8,96,128]{2,1,0:T(8,128)} custom-call(f32[8,96,128]{2,1,0:T(8,128)} %reshape.38.x_ref), custom_call_target="tpu_custom_call" | custom-call | tf_op jit(solution)/shard_map/exchange/pallas_call | solution.py:482
  58.9 1.4 %reshape.39 = f32[2,4,8,2,3,8,32]{6,5,4,3,2,1,0:T(8,128)S(1)} reshape(f32[8,96,128]{2,1,0:T(8,128)} %exchange.1) | data formatting | bytes 786432 | tf_op jit(solution)/shard_map/reshape | solution.py:612
  60.2 0.0 copy-done.1
  60.2 1.4 %fusion.9 = f32[64,8,2,3,32]{0,4,1,3,2:T(8,128)S(1)} fusion(f32[2,2,2,4,8,64,1,1]{5,4,0,6,7,1,3,2:T(8,128)S(1)} %copy-done.1, f32[2,4,8,2,3,8,32]{6,5,4,3,2,1,0:T(8,128)S(1)} %reshape.39), kind=kOutput, calls=%fused_computation.7 | convolution fusion | flops 75497472 | bytes 851968 | tf_op jit(solution)/shard_map/abzpcyx,pqabyk->kzqcx/dot_general | solution.py:615
  61.7 2.3 %copy.21 = f32[64,8,2,3,32]{4,3,2,1,0:T(4,128)S(1)} copy(f32[64,8,2,3,32]{0,4,1,3,2:T(8,128)S(1)} %fusion.9) | data formatting | bytes 786432 | tf_op jit(solution)/shard_map/abzpcyx,pqabyk->kzqcx/transpose | solution.py:615
  64.0 2.0 %all_to_all.12 = f32[4,16,1536]{2,1,0:T(8,128)} reshape(f32[64,8,2,3,32]{4,3,2,1,0:T(4,128)S(1)} %copy.21) | data formatting | bytes 786432 | tf_op jit(solution)/shard_map/all_to_all | solution.py:617
  66.0 3.5 %all-to-all-start = ((f32[4,16,1536]{2,1,0:T(8,128)}), f32[4,16,1536]{2,1,0:T(8,128)S(1)}, u32[]{:S(2)}, u32[]{:S(2)}) async-start(f32[4,16,1536]{2,1,0:T(8,128)} %all_to_all.12), calls=%async_computation | async-start | bytes 786432 | tf_op jit(solution)/shard_map/all_to_all | solution.py:617
  69.4 11.2 %collide.1 = f32[3,81920]{1,0:T(4,128)} custom-call(s32[3]{0:T(128)} %shift_ref.3, s32[640,128]{1,0:T(8,128)} %bitcast.54, f32[3,81920]{1,0:T(4,128)} %v_ref.3, f32[2,2,6,128,128]{4,3,2,1,0:T(8,128)} %get-tuple-element.5.tab_ref), custom_call_target="tpu_custom_call" | custom-call | flops 14745600 | bytes 4000000 | tf_op jit(solution)/shard_map/collide/pallas_call | solution.py:432
  80.7 0.0 copy-start
  80.7 0.0 all-to-all-done
  80.7 1.3 %reshape.40 = f32[16,4,8,2,3,32]{5,4,3,2,0,1:T(4,128)S(1)} reshape(f32[16,4,1536]{2,0,1:T(8,128)S(1)} %bitcast.51) | data formatting | bytes 786432 | tf_op jit(solution)/shard_map/reshape | solution.py:619
  82.0 0.0 copy-done
  82.0 0.9 fusion.12
  82.9 0.9 copy.24
  83.8 11.9 %shells.1 = f32[8,128]{1,0:T(8,128)} custom-call(f32[2,3,128,128]{3,2,1,0:T(8,128)} %bitcast.52, f32[8,128]{1,0:T(8,128)} %constant.11.clone.n_ref), custom_call_target="tpu_custom_call" | custom-call | tf_op jit(solution)/shard_map/shells/pallas_call | solution.py:566
  95.7 1.2 %slice_bitcast_fusion = f32[32]{0:T(128)} fusion(f32[8,128]{1,0:T(8,128)} %shells.1), kind=kLoop, calls=%fused_computation.10 | loop fusion | bytes 256 | tf_op jit(solution)/shard_map/squeeze | solution.py:581
Async XLA Ops:
  17.1 26.2 %copy-start.2 = (f32[4,16,64,2,1,1]{2,1,0,5,4,3:T(8,128)S(1)}, f32[4,16,64,2,1,1]{2,1,0,5,4,3:T(8,128)}, u32[]{:S(2)}) copy-start(f32[4,16,64,2,1,1]{2,1,0,5,4,3:T(8,128)} %constant.12) | copy-start | bytes 98308
  46.3 14.0 %copy-start.1 = (f32[2,2,2,4,8,64,1,1]{5,4,0,6,7,1,3,2:T(8,128)S(1)}, f32[2,2,2,4,8,64,1,1]{5,4,0,6,7,1,3,2:T(8,128)}, u32[]{:S(2)}) copy-start(f32[2,2,2,4,8,64,1,1]{5,4,0,6,7,1,3,2:T(8,128)} %constant.14) | copy-start | bytes 196612
  66.0 14.7 %all-to-all-start = ((f32[4,16,1536]{2,1,0:T(8,128)}), f32[4,16,1536]{2,1,0:T(8,128)S(1)}, u32[]{:S(2)}, u32[]{:S(2)}) async-start(f32[4,16,1536]{2,1,0:T(8,128)} %all_to_all.12), calls=%async_computation | async-start | bytes 786432 | tf_op jit(solution)/shard_map/all_to_all | solution.py:617
  80.7 1.3 %copy-start = (f32[2,2,4,32,128,1,1]{4,3,0,2,1,6,5:T(8,128)S(1)}, f32[2,2,4,32,128,1,1]{4,3,0,2,1,6,5:T(8,128)}, u32[]{:S(2)}) copy-start(f32[2,2,4,32,128,1,1]{4,3,0,2,1,6,5:T(8,128)} %constant.15) | copy-start | bytes 786436

commit v3 on v2

--- a/solution.py
+++ b/solution.py
@@ -334,10 +334,12 @@
         cell_ref[lax.rem(me_z + count_z - step, count_z)] = incoming[step - 1]
 
 
-def collide_kernel(shift_ref, place_ref, v_ref, tab_ref, out_ref):
+def collide_group(group, shift_ref, place_ref, v_ref, tab_ref, out_ref):
     sub = iota((8, TILE), 0)
+    tiles = pl.ds(pl.multiple_of(group * 8, 8), 8)
+    base = group * (8 * PPC * TILE)
     for chunk in range(PPC):
-        place = place_ref[pl.ds(chunk, 8, stride=PPC), :]
+        place = place_ref[pl.ds(group * (8 * PPC) + chunk, 8, stride=PPC), :]
         bit_x, bit_y, bit_z = shift_bits(place, shift_ref)
         cell = place >> 6
         x_new = (cell >> 4) + bit_x
@@ -348,24 +350,24 @@
         upper = bit_y == 1
         got = []
         for c in range(6):
-            low = jnp.where(outside, take(tab_ref[0, 1, c], index), take(tab_ref[0, 0, c], index))
-            high = jnp.where(outside, take(tab_ref[1, 1, c], index), take(tab_ref[1, 0, c], index))
+            low = jnp.where(outside, take(tab_ref[0, 1, c, tiles, :], index), take(tab_ref[0, 0, c, tiles, :], index))
+            high = jnp.where(outside, take(tab_ref[1, 1, c, tiles, :], index), take(tab_ref[1, 0, c, tiles, :], index))
             got.append(jnp.where(upper, high, low))
         speed = []
         for c in range(3):
             value = jnp.zeros((8, TILE), F32)
             for tile in range(8):
-                at = (tile * PPC + chunk) * TILE
+                at = pl.ds(pl.multiple_of(base + (tile * PPC + chunk) * TILE, TILE), TILE)
                 value = jnp.where(
-                    sub == tile, jnp.broadcast_to(v_ref[c : c + 1, at : at + TILE], (8, TILE)), value
+                    sub == tile, jnp.broadcast_to(v_ref[c : c + 1, at], (8, TILE)), value
                 )
             speed.append(value)
         turned = rotate([speed[c] - got[c] for c in range(3)], got[3:6])
         for c in range(3):
             value = got[c] + turned[c]
             for tile in range(8):
-                at = (tile * PPC + chunk) * TILE
-                out_ref[c : c + 1, at : at + TILE] = value[tile : tile + 1]
+                at = pl.ds(pl.multiple_of(base + (tile * PPC + chunk) * TILE, TILE), TILE)
+                out_ref[c : c + 1, at] = value[tile : tile + 1]
 
 
 def deposit(grid_shift, place, velocity, tiles):
@@ -427,24 +429,6 @@
     )(sums, axis)
 
 
-def collide_particles(grid_shift, place, velocity, tables, tiles):
-    rows = 8 * PPC
-    return pl.pallas_call(
-        collide_kernel,
-        grid=(tiles // 8,),
-        in_specs=[
-            pl.BlockSpec(memory_space=pltpu.SMEM),
-            pl.BlockSpec((rows, TILE), lambda i: (i, 0)),
-            pl.BlockSpec((3, rows * TILE), lambda i: (0, i)),
-            pl.BlockSpec((2, 2, 6, 8, TILE), lambda i: (0, 0, 0, i, 0)),
-        ],
-        out_specs=pl.BlockSpec((3, rows * TILE), lambda i: (0, i)),
-        out_shape=jax.ShapeDtypeStruct(velocity.shape, F32),
-        cost_estimate=pl.CostEstimate(flops=60 * velocity.size, bytes_accessed=4000000, transcendentals=0),
-        name="collide",
-    )(grid_shift, place, velocity, tables)
-
-
 def exchange_kernel(x_ref, out_ref, send_sem, recv_sem):
     count_y, count_z = lax.axis_size("gy"), lax.axis_size("gz")
     me_y, me_z = lax.axis_index("gy"), lax.axis_index("gz")
@@ -490,7 +474,19 @@
     )(blocks)
 
 
-def shell_kernel(lengths, shells, m_ref, n_ref, out_ref, bins, mine, others, send_sem, recv_sem):
+def final_kernel(
+    lengths, shells, shift_ref, place_ref, v_ref, tab_ref, block_ref, phase_ref, n_ref,
+    new_ref, m_ref, out_ref,
+    arrived, bins, mine, others, block_send, block_recv, send_sem, recv_sem,
+):
+    groups = place_ref.shape[0] // (8 * PPC)
+    cuts = [0, groups // 4, groups * 3 // 4, groups]
+
+    def collide_some(part):
+        @pl.loop(cuts[part], cuts[part + 1])
+        def _(group):
+            collide_group(group, shift_ref, place_ref, v_ref, tab_ref, new_ref)
+
     names = ("gx", "gy", "gz")
     sizes = [lax.axis_size(name) for name in names]
     at = [lax.axis_index(name) for name in names]
@@ -507,14 +503,42 @@
         pl.semaphore_signal(
             barrier, inc=1, device_id=peer, device_id_type=pl.DeviceIdType.MESH
         )
+    collide_some(0)
+    pl.semaphore_wait(barrier, len(peers))
+    blocks = []
+    for step in range(1, sizes[0]):
+        target = lax.rem(at[0] + step, sizes[0])
+        copy = pltpu.make_async_remote_copy(
+            src_ref=block_ref.at[target], dst_ref=arrived.at[step - 1],
+            send_sem=block_send.at[step - 1], recv_sem=block_recv.at[step - 1],
+            device_id={"gx": target}, device_id_type=pl.DeviceIdType.MESH,
+        )
+        copy.start()
+        blocks.append(copy)
+    collide_some(1)
+    for copy in blocks:
+        copy.wait()
     length_x, length_y, length_z = lengths
-    rows = m_ref.shape[2]
+    half = block_ref.shape[1]
+    modes = jnp.zeros((half, 4 * length_x), F32)
+    for step in range(sizes[0]):
+        source = lax.rem(at[0] + sizes[0] - step, sizes[0])
+        value = arrived[step - 1] if step else block_ref[source]
+        high = value.astype(jnp.bfloat16)
+        low = (value - high.astype(F32)).astype(jnp.bfloat16)
+        for left, right in ((high, 0), (low, 0), (high, 1)):
+            modes = modes + jnp.dot(left, phase_ref[right, source], preferred_element_type=F32)
+    for h in range(2):
+        for part in range(2):
+            at_lane = (2 * h + part) * length_x
+            m_ref[part, h * half : (h + 1) * half, :] = modes[:, at_lane : at_lane + length_x]
+    rows = 2 * half // 3
     depth_y = length_y // sizes[0]
     depth_z = length_z // (sizes[1] * sizes[2])
     energy = jnp.zeros((rows, length_x), F32)
     for part in range(2):
         for c in range(3):
-            value = m_ref[part, c]
+            value = m_ref[part, c * rows : (c + 1) * rows, :]
             energy = energy + value * value
     row = iota((rows, length_x), 0)
     kz = (at[1] * sizes[2] + at[2]) * depth_z + lax.div(row, depth_y)
@@ -536,7 +560,6 @@
     line = jnp.sum(jnp.where(diagonal, column, 0.0), axis=0, keepdims=True)
     packed = jnp.broadcast_to(line, (8, width))
     mine[...] = packed
-    pl.semaphore_wait(barrier, len(peers))
     copies = [
         pltpu.make_async_remote_copy(
             src_ref=mine, dst_ref=others.at[slot], send_sem=send_sem.at[slot],
@@ -546,39 +569,49 @@
     ]
     for copy in copies:
         copy.start()
+    collide_some(2)
     for copy in copies:
         copy.wait()
     total = packed + jnp.sum(others[...], axis=0)
     out_ref[...] = total / n_ref[...]
 
 
-def shell_spectrum(modes, lengths):
+def finish(grid_shift, place, velocity, tables, blocks, phases, lengths):
     shells = min(lengths) // 2
     width = lengths[0]
-    count = lax.axis_size("gx") * lax.axis_size("gy") * lax.axis_size("gz")
+    count_x = lax.axis_size("gx")
+    count = count_x * lax.axis_size("gy") * lax.axis_size("gz")
     dma = pltpu.SemaphoreType.DMA
-    rows = modes.reshape(2, 3, -1, width)
+    half = blocks.shape[1]
     waves = [np.minimum(np.arange(n), n - np.arange(n)) ** 2 for n in lengths]
     square = waves[2][:, None, None] + waves[1][None, :, None] + waves[0][None, None, :]
     shell = np.floor(np.sqrt(square.astype(np.float64))).astype(np.int64).ravel()
     number = np.ones((8, width), np.float32)
     number[:, :shells] = np.bincount(shell, minlength=shells)[:shells]
-    out = pl.pallas_call(
-        functools.partial(shell_kernel, lengths, shells),
-        in_specs=[pl.BlockSpec(memory_space=VMEM)] * 2,
-        out_specs=pl.BlockSpec(memory_space=VMEM),
-        out_shape=jax.ShapeDtypeStruct((8, width), F32),
+    whole = pl.BlockSpec(memory_space=VMEM)
+    new_velocity, modes, out = pl.pallas_call(
+        functools.partial(final_kernel, lengths, shells),
+        in_specs=[pl.BlockSpec(memory_space=pltpu.SMEM)] + [whole] * 6,
+        out_specs=[whole] * 3,
+        out_shape=[
+            jax.ShapeDtypeStruct(velocity.shape, F32),
+            jax.ShapeDtypeStruct((2, 2 * half, width), F32),
+            jax.ShapeDtypeStruct((8, width), F32),
+        ],
         scratch_shapes=[
+            VMEM((count_x - 1, half, blocks.shape[2]), F32),
             VMEM((shells, width), F32),
             VMEM((8, width), F32),
             VMEM((count - 1, 8, width), F32),
+            dma((count_x - 1,)),
+            dma((count_x - 1,)),
             dma((count - 1,)),
             dma((count - 1,)),
         ],
         compiler_params=pltpu.CompilerParams(collective_id=1, has_side_effects=True),
-        name="shells",
-    )(rows, jnp.asarray(number))
-    return out[0, :shells]
+        name="finish",
+    )(grid_shift, place, velocity, tables, blocks, phases, jnp.asarray(number))
+    return new_velocity, modes, out[0, :shells]
 
 
 def phase_tables(positions, length):
@@ -595,7 +628,6 @@
     sums = deposit(grid_shift, place, velocity, tile_count)
     axis = rotation_axis.reshape(tile_count, TILE).astype(F32)
     tables, cell_sums = halo(sums.reshape(4, 2, 2, 2, tile_count, TILE), axis, tile_count)
-    new_velocity = collide_particles(grid_shift, place, velocity, tables, tile_count)
     count_x = lax.axis_size("gx")
     count_y = lax.axis_size("gy")
     count_z = lax.axis_size("gz")
@@ -612,18 +644,26 @@
     pencil = pencil.reshape(count_y, count_z, depth_z, 2, 3, rows_y, size_x)
     cos_y, sin_y = phase_tables(np.arange(length_y).reshape(count_y, count_z, rows_y), length_y)
     both_y = np.stack([np.stack([cos_y, -sin_y]), np.stack([sin_y, cos_y])])
-    stacked_y = jnp.einsum("abzpcyx,pqabyk->kzqcx", pencil, both_y, precision=HIGH)
-    stacked_y = stacked_y.reshape(length_y, depth_z * 6 * size_x)
-    columns = lax.all_to_all(stacked_y, "gx", split_axis=0, concat_axis=1, tiled=True)
     depth_y = length_y // count_x
-    columns = columns.reshape(depth_y, count_x, depth_z, 2, 3, size_x)
+    half = 3 * depth_z * depth_y // 2
+    stacked_y = jnp.einsum("abzpcyx,pqabyk->czkqx", pencil, both_y, precision=HIGH)
+    blocks = stacked_y.reshape(3, depth_z, count_x, depth_y, 2 * size_x)
+    blocks = blocks.transpose(2, 0, 1, 3, 4).reshape(count_x, 2, half, 2 * size_x)
+    blocks = blocks.transpose(0, 2, 1, 3).reshape(count_x, half, 4 * size_x)
     cos_x, sin_x = phase_tables(np.arange(length_x).reshape(count_x, size_x), length_x)
     norm_scale = 1.0 / math.sqrt(length_x * length_y * length_z)
-    both_x = np.stack([np.stack([cos_x, -sin_x]), np.stack([sin_x, cos_x])])
-    both_x = (both_x * norm_scale).astype(np.float32)
-    modes = jnp.einsum("ygzpcx,pqgxk->qczyk", columns, both_x, precision=HIGH)
-    spectrum = shell_spectrum(modes, (length_x, length_y, length_z))
-    return (new_velocity, modes, spectrum)
+    both_x = np.stack([np.stack([cos_x, -sin_x]), np.stack([sin_x, cos_x])]) * norm_scale
+    both_x = both_x.transpose(2, 0, 3, 1, 4).reshape(count_x, 2 * size_x, 2 * length_x)
+    phases = np.zeros((count_x, 4 * size_x, 4 * length_x), np.float32)
+    phases[:, : 2 * size_x, : 2 * length_x] = both_x
+    phases[:, 2 * size_x :, 2 * length_x :] = both_x
+    high = phases.astype(jnp.bfloat16)
+    low = (phases - high.astype(np.float32)).astype(jnp.bfloat16)
+    new_velocity, modes, spectrum = finish(
+        grid_shift, place, velocity, tables, blocks, jnp.asarray(np.stack([high, low])),
+        (length_x, length_y, length_z),
+    )
+    return (new_velocity, modes.reshape(2, 3, depth_z, depth_y, length_x), spectrum)
 
 
 def solution(mesh):

time: 98.4 us -> 91.1 us (0.926)
  starting transfers between devices: 3.46 us -> 0 us
  Pallas kernels: 75 us -> 72.6 us
    all_to_all x1 -> x0, starting transfers between devices: 3.46 us -> none  [per_device(): lax.all_to_all(stacked_y, 'gx', split_axis=0, concat_axis=1, tiled=True)]
    unnamed x7 -> x8, local copies, waits for them, and re-layouts: 0.88 us -> 3.35 us
    pallas_call x2 -> x1, Pallas kernels: 23.2 us -> 20.7 us  [finish(): pl.pallas_call(functools.partial(final_kernel, lengths, shells), in_specs...]
    all_to_all x1 -> x0, local copies, waits for them, and re-layouts: 1.96 us -> none  [per_device(): lax.all_to_all(stacked_y, 'gx', split_axis=0, concat_axis=1, tiled=True)]
    transpose x1 -> x3, local copies, waits for them, and re-layouts: 2.34 us -> 1.27 us  [the longest x1 0.88 us: per_device(): jnp.einsum('abzpcyx,pqabyk->czkqx', pencil, both_y, precision=HIGH)]
    dot_general x2 -> x1, matrix products: 2.34 us -> 1.42 us  [per_device(): jnp.einsum('abzpcyx,pqabyk->czkqx', pencil, both_y, precision=HIGH)]
  transfers between devices with their start and end apart: 1 -> 0, of which waited for: 0 -> 0; matrix products, arithmetic and copies ran while one was open for 0% -> 0% of each run, Pallas kernels for 12% -> 0%
where the time goes in v3:
time: 91.1 us; the launch traced here: 90.1 us
  Pallas kernels  72.6 us (80%)
  local copies, waits for them, and re-layouts  13.3 us (15%)
  matrix products  2.52 us (3%)
  other arithmetic  0.97 us (1%)
    pallas_call x1, Pallas kernels, halo(): pl.pallas_call(halo_kernel, in_specs=[pl.BlockSpec(memory_space=VMEM)] *...  24.8 us
    pallas_call x1, Pallas kernels, finish(): pl.pallas_call(functools.partial(final_kernel, lengths, shells), in_specs...  20.7 us
    pallas_call x1, Pallas kernels, deposit(): pl.pallas_call(deposit_kernel, grid=(tiles // 8,), in_specs=[pl.BlockSpec...  14.4 us
    pallas_call x1, Pallas kernels, exchange(): pl.pallas_call(exchange_kernel, in_specs=[pl.BlockSpec(memory_space=VMEM)...  12.6 us
    unnamed x8, local copies, waits for them, and re-layouts  3.35 us

profile of v3, /device:TPU:0, one launch (start us, length us, event | category | flops | bytes accessed | tf_op | source)
XLA Modules:
  0.0 90.1 jit_solution(13384678681195364441)
XLA Ops:
  0.6 1.0 %convert_element_type.5 = f32[32,32,16]{1,2,0:T(8,128)S(1)} convert(s32[32,32,16]{1,2,0:T(8,128)} %param.11) | non-fusion elementwise | flops 16384 | bytes 131072 | tf_op jit(solution)/shard_map/convert_element_type | solution.py:629
  1.6 0.2 copy.15
  1.8 0.8 convert_element_type.6.a_ref
  2.6 14.4 %deposit.1 = f32[4,8,128,128]{3,2,1,0:T(8,128)} custom-call(s32[3]{0:T(128)} %shift_ref.3, s32[640,128]{1,0:T(8,128)} %bitcast.44, f32[3,81920]{1,0:T(4,128)} %v_ref.3), custom_call_target="tpu_custom_call" | custom-call | tf_op jit(solution)/shard_map/deposit/pallas_call | solution.py:375
  17.1 0.0 copy-start.2
  17.1 24.8 %halo.1 = (f32[2,2,6,128,128]{4,3,2,1,0:T(8,128)}, f32[4,3,32,128]{3,2,1,0:T(8,128)}) custom-call(f32[4,2,2,2,128,128]{5,4,3,2,1,0:T(8,128)} %bitcast.40, f32[128,128]{1,0:T(8,128)} %convert_element_type.6.a_ref), custom_call_target="tpu_custom_call" | custom-call | tf_op jit(solution)/shard_map/halo/pallas_call | solution.py:393
  41.9 1.4 %reshape.37 = f32[4,3,8,32,16]{4,3,2,1,0:T(8,128)S(1)} reshape(f32[4,3,32,128]{3,2,1,0:T(8,128)} %get-tuple-element.9) | data formatting | bytes 393216 | tf_op jit(solution)/shard_map/reshape | solution.py:638
  43.3 0.0 copy-done.2
  43.3 1.1 %fusion.4 = f32[64,2,3,8,32]{0,4,3,2,1:T(8,128)S(1)} fusion(f32[4,3,8,32,16]{4,3,2,1,0:T(8,128)S(1)} %reshape.37, f32[4,16,64,2,1,1]{2,1,0,5,4,3:T(8,128)S(1)} %copy-done.2), kind=kOutput, calls=%fused_computation.4 | convolution fusion | flops 37748736 | bytes 622592 | tf_op jit(solution)/shard_map/gcyxz,gzkp->kpcyx/dot_general | solution.py:641
  44.4 0.7 copy.17
  45.1 1.1 %reshape.38.x_ref = f32[8,96,128]{2,1,0:T(8,128)} reshape(f32[64,2,3,8,32]{4,3,2,1,0:T(8,128)S(1)} %copy.17) | data formatting | bytes 786432 | tf_op jit(solution)/shard_map/reshape | solution.py:643
  46.3 0.0 copy-start.1
  46.3 12.6 %exchange.1 = f32[8,96,128]{2,1,0:T(8,128)} custom-call(f32[8,96,128]{2,1,0:T(8,128)} %reshape.38.x_ref), custom_call_target="tpu_custom_call" | custom-call | tf_op jit(solution)/shard_map/exchange/pallas_call | solution.py:466
  58.9 1.4 %reshape.39 = f32[2,4,8,2,3,8,32]{6,5,4,3,2,1,0:T(8,128)S(1)} reshape(f32[8,96,128]{2,1,0:T(8,128)} %exchange.1) | data formatting | bytes 786432 | tf_op jit(solution)/shard_map/reshape | solution.py:644
  60.2 0.0 copy-done.1
  60.2 1.4 %fusion.7 = f32[3,8,64,2,32]{2,4,1,0,3:T(8,128)S(1)} fusion(f32[2,2,2,4,8,64,1,1]{5,4,0,6,7,1,3,2:T(8,128)S(1)} %copy-done.1, f32[2,4,8,2,3,8,32]{6,5,4,3,2,1,0:T(8,128)S(1)} %reshape.39), kind=kOutput, calls=%fused_computation.5 | convolution fusion | flops 75497472 | bytes 851968 | tf_op jit(solution)/shard_map/abzpcyx,pqabyk->czkqx/dot_general | solution.py:649
  61.7 0.9 copy.19
  62.6 0.9 reshape.40
  63.4 0.1 copy.20
  63.5 0.3 copy.21
  63.8 0.9 %copy.22.block_ref = f32[4,192,128]{2,1,0:T(8,128)} copy(f32[4,192,128]{1,2,0:T(8,128)S(1)} %bitcast.43) | data formatting | bytes 786432 | tf_op jit(solution)/shard_map/reshape | solution.py:652
  64.8 20.7 %finish.1 = (f32[3,81920]{1,0:T(4,128)}, f32[2,384,128]{2,1,0:T(8,128)}, f32[8,128]{1,0:T(8,128)}) custom-call(s32[3]{0:T(128)} %shift_ref.3, s32[640,128]{1,0:T(8,128)} %bitcast.45, f32[3,81920]{1,0:T(4,128)} %v_ref.3, f32[2,2,6,128,128]{4,3,2,1,0:T(8,128)} %get-tuple-element.8.tab_ref, f32[4,192,128]{2,1,0:T(8,128)} %copy.22.block_ref, ...), custom_call_target="tpu_custom_call" | custom-call | tf_op jit(solution)/shard_map/finish/pallas_call | solution.py:592
  85.5 0.0 copy-start
  85.5 1.2 %slice_bitcast_fusion = f32[32]{0:T(128)} fusion(f32[8,128]{1,0:T(8,128)} %get-tuple-element.12), kind=kLoop, calls=%fused_computation.7 | loop fusion | bytes 256 | tf_op jit(solution)/shard_map/squeeze | solution.py:614
  86.7 2.6 %copy.40 = f32[3,81920]{1,0:T(4,128)} copy(f32[3,81920]{1,0:T(4,128)} %get-tuple-element.16) | data formatting | bytes 1966080
  89.3 0.0 copy-done
  89.3 0.7 copy.41
Async XLA Ops:
  17.1 26.2 %copy-start.2 = (f32[4,16,64,2,1,1]{2,1,0,5,4,3:T(8,128)S(1)}, f32[4,16,64,2,1,1]{2,1,0,5,4,3:T(8,128)}, u32[]{:S(2)}) copy-start(f32[4,16,64,2,1,1]{2,1,0,5,4,3:T(8,128)} %constant.12) | copy-start | bytes 98308
  46.3 14.0 %copy-start.1 = (f32[2,2,2,4,8,64,1,1]{5,4,0,6,7,1,3,2:T(8,128)S(1)}, f32[2,2,2,4,8,64,1,1]{5,4,0,6,7,1,3,2:T(8,128)}, u32[]{:S(2)}) copy-start(f32[2,2,2,4,8,64,1,1]{5,4,0,6,7,1,3,2:T(8,128)} %constant.14) | copy-start | bytes 196612
  85.5 3.8 %copy-start = (f32[2,384,128]{2,1,0:T(8,128)S(1)}, f32[2,384,128]{2,1,0:T(8,128)}, u32[]{:S(2)}) copy-start(f32[2,384,128]{2,1,0:T(8,128)} %get-tuple-element.11) | copy-start | bytes 1179652

commit v4 on v3

--- a/solution.py
+++ b/solution.py
@@ -37,9 +37,11 @@
     place = place_ref[...]
     bit_x, bit_y, bit_z = shift_bits(place, shift_ref)
     octant = bit_x * 4 + bit_y * 2 + bit_z
-    member = place >> 6
+    member = (place >> 6).astype(F32).astype(jnp.bfloat16)
     sub8 = iota((8, TILE), 0)
-    cells = iota((TILE, TILE), 0)
+    cells = iota((TILE, TILE), 0).astype(F32).astype(jnp.bfloat16)
+    one = jnp.ones((), jnp.bfloat16)
+    zero = jnp.zeros((), jnp.bfloat16)
     for tile in range(8):
         lhs = []
         hots = []
@@ -57,7 +59,7 @@
             parts.append(jnp.zeros((8, TILE), F32))
             lhs.append(jnp.concatenate(parts, axis=0).astype(jnp.bfloat16))
             hot = jnp.broadcast_to(member[row : row + 1], (TILE, TILE)) == cells
-            hots.append(jnp.where(hot, 1.0, 0.0).astype(jnp.bfloat16))
+            hots.append(jnp.where(hot, one, zero))
         sums = lax.dot_general(
             jnp.concatenate(lhs, axis=1),
             jnp.concatenate(hots, axis=1),
@@ -429,7 +431,9 @@
     )(sums, axis)
 
 
-def exchange_kernel(x_ref, out_ref, send_sem, recv_sem):
+def exchange_kernel(
+    shift_ref, place_ref, v_ref, tab_ref, x_ref, out_ref, new_ref, send_sem, recv_sem
+):
     count_y, count_z = lax.axis_size("gy"), lax.axis_size("gz")
     me_y, me_z = lax.axis_index("gy"), lax.axis_index("gz")
     me = me_y * count_z + me_z
@@ -456,31 +460,39 @@
     for copy in copies:
         copy.start()
     out_ref[me] = x_ref[me]
+
+    @pl.loop(0, place_ref.shape[0] // (16 * PPC))
+    def _(group):
+        collide_group(group, shift_ref, place_ref, v_ref, tab_ref, new_ref)
+
     for copy in copies:
         copy.wait()
 
 
-def exchange(blocks):
+def exchange(grid_shift, place, velocity, tables, blocks):
     peers = blocks.shape[0] - 1
     dma = pltpu.SemaphoreType.DMA
     return pl.pallas_call(
         exchange_kernel,
-        in_specs=[pl.BlockSpec(memory_space=VMEM)],
-        out_specs=pl.BlockSpec(memory_space=VMEM),
-        out_shape=jax.ShapeDtypeStruct(blocks.shape, F32),
+        in_specs=particle_specs() + [pl.BlockSpec(memory_space=VMEM)],
+        out_specs=[pl.BlockSpec(memory_space=VMEM)] * 2,
+        out_shape=[
+            jax.ShapeDtypeStruct(blocks.shape, F32),
+            jax.ShapeDtypeStruct((3, velocity.shape[1] // 2), F32),
+        ],
         scratch_shapes=[dma((peers,)), dma((peers,))],
         compiler_params=pltpu.CompilerParams(collective_id=2, has_side_effects=True),
         name="exchange",
-    )(blocks)
+    )(grid_shift, place, velocity, tables, blocks)
 
 
 def final_kernel(
-    lengths, shells, shift_ref, place_ref, v_ref, tab_ref, block_ref, phase_ref, n_ref,
+    lengths, shells, shift_ref, place_ref, v_ref, tab_ref, done_ref, block_ref, phase_ref, n_ref,
     new_ref, m_ref, out_ref,
     arrived, bins, mine, others, block_send, block_recv, send_sem, recv_sem,
 ):
     groups = place_ref.shape[0] // (8 * PPC)
-    cuts = [0, groups // 4, groups * 3 // 4, groups]
+    cuts = [groups // 2, groups * 5 // 8, groups * 7 // 8, groups]
 
     def collide_some(part):
         @pl.loop(cuts[part], cuts[part + 1])
@@ -504,6 +516,7 @@
             barrier, inc=1, device_id=peer, device_id_type=pl.DeviceIdType.MESH
         )
     collide_some(0)
+    new_ref[:, 0 : done_ref.shape[1]] = done_ref[...]
     pl.semaphore_wait(barrier, len(peers))
     blocks = []
     for step in range(1, sizes[0]):
@@ -576,7 +589,13 @@
     out_ref[...] = total / n_ref[...]
 
 
-def finish(grid_shift, place, velocity, tables, blocks, phases, lengths):
+def particle_specs():
+    return [
+        pl.BlockSpec(memory_space=pltpu.SMEM),
+    ] + [pl.BlockSpec(memory_space=VMEM)] * 3
+
+
+def finish(grid_shift, place, velocity, tables, done, blocks, phases, lengths):
     shells = min(lengths) // 2
     width = lengths[0]
     count_x = lax.axis_size("gx")
@@ -591,7 +610,7 @@
     whole = pl.BlockSpec(memory_space=VMEM)
     new_velocity, modes, out = pl.pallas_call(
         functools.partial(final_kernel, lengths, shells),
-        in_specs=[pl.BlockSpec(memory_space=pltpu.SMEM)] + [whole] * 6,
+        in_specs=particle_specs() + [whole] * 4,
         out_specs=[whole] * 3,
         out_shape=[
             jax.ShapeDtypeStruct(velocity.shape, F32),
@@ -610,7 +629,7 @@
         ],
         compiler_params=pltpu.CompilerParams(collective_id=1, has_side_effects=True),
         name="finish",
-    )(grid_shift, place, velocity, tables, blocks, phases, jnp.asarray(number))
+    )(grid_shift, place, velocity, tables, done, blocks, phases, jnp.asarray(number))
     return new_velocity, modes, out[0, :shells]
 
 
@@ -640,7 +659,8 @@
     both_z = np.stack([cos_z, -sin_z], axis=-1)
     stacked_z = jnp.einsum("gcyxz,gzkp->kpcyx", arrived, both_z, precision=HIGH)
     depth_z = length_z // (count_y * count_z)
-    pencil = exchange(stacked_z.reshape(count_y * count_z, -1, TILE))
+    blocks = stacked_z.reshape(count_y * count_z, -1, TILE)
+    pencil, done = exchange(grid_shift, place, velocity, tables, blocks)
     pencil = pencil.reshape(count_y, count_z, depth_z, 2, 3, rows_y, size_x)
     cos_y, sin_y = phase_tables(np.arange(length_y).reshape(count_y, count_z, rows_y), length_y)
     both_y = np.stack([np.stack([cos_y, -sin_y]), np.stack([sin_y, cos_y])])
@@ -660,7 +680,7 @@
     high = phases.astype(jnp.bfloat16)
     low = (phases - high.astype(np.float32)).astype(jnp.bfloat16)
     new_velocity, modes, spectrum = finish(
-        grid_shift, place, velocity, tables, blocks, jnp.asarray(np.stack([high, low])),
+        grid_shift, place, velocity, tables, done, blocks, jnp.asarray(np.stack([high, low])),
         (length_x, length_y, length_z),
     )
     return (new_velocity, modes.reshape(2, 3, depth_z, depth_y, length_x), spectrum)

time: 91.1 us -> 92.6 us (1.016)
  Pallas kernels: 72.6 us -> 74 us
    pallas_call x1, Pallas kernels: 12.6 us -> 13.8 us  [exchange(): pl.pallas_call(exchange_kernel, in_specs=particle_specs() + [pl.BlockSpec...]
where the time goes in v4:
time: 92.6 us; the launch traced here: 91.6 us
  Pallas kernels  74 us (80%)
  local copies, waits for them, and re-layouts  13.3 us (14%)
  matrix products  2.52 us (3%)
  other arithmetic  0.97 us (1%)
    pallas_call x1, Pallas kernels, halo(): pl.pallas_call(halo_kernel, in_specs=[pl.BlockSpec(memory_space=VMEM)] *...  24.8 us
    pallas_call x1, Pallas kernels, finish(): pl.pallas_call(functools.partial(final_kernel, lengths, shells), in_specs...  20.9 us
    pallas_call x1, Pallas kernels, deposit(): pl.pallas_call(deposit_kernel, grid=(tiles // 8,), in_specs=[pl.BlockSpec...  14.5 us
    pallas_call x1, Pallas kernels, exchange(): pl.pallas_call(exchange_kernel, in_specs=particle_specs() + [pl.BlockSpec...  13.8 us
    unnamed x8, local copies, waits for them, and re-layouts  3.36 us

profile of v4, /device:TPU:0, one launch (start us, length us, event | category | flops | bytes accessed | tf_op | source)
XLA Modules:
  0.0 91.6 jit_solution(11229637044887160479)
XLA Ops:
  0.6 1.0 %convert_element_type.5 = f32[32,32,16]{1,2,0:T(8,128)S(1)} convert(s32[32,32,16]{1,2,0:T(8,128)} %param.11) | non-fusion elementwise | flops 16384 | bytes 131072 | tf_op jit(solution)/shard_map/convert_element_type | solution.py:648
  1.6 0.2 copy.15
  1.8 0.8 convert_element_type.6.a_ref
  2.6 14.5 %deposit.1 = f32[4,8,128,128]{3,2,1,0:T(8,128)} custom-call(s32[3]{0:T(128)} %shift_ref.5, s32[640,128]{1,0:T(8,128)} %bitcast.43, f32[3,81920]{1,0:T(4,128)} %v_ref.5), custom_call_target="tpu_custom_call" | custom-call | tf_op jit(solution)/shard_map/deposit/pallas_call | solution.py:377
  17.1 0.0 copy-start.2
  17.1 24.8 %halo.1 = (f32[2,2,6,128,128]{4,3,2,1,0:T(8,128)}, f32[4,3,32,128]{3,2,1,0:T(8,128)}) custom-call(f32[4,2,2,2,128,128]{5,4,3,2,1,0:T(8,128)} %bitcast.40, f32[128,128]{1,0:T(8,128)} %convert_element_type.6.a_ref), custom_call_target="tpu_custom_call" | custom-call | tf_op jit(solution)/shard_map/halo/pallas_call | solution.py:395
  42.0 1.4 %reshape.37 = f32[4,3,8,32,16]{4,3,2,1,0:T(8,128)S(1)} reshape(f32[4,3,32,128]{3,2,1,0:T(8,128)} %get-tuple-element.11) | data formatting | bytes 393216 | tf_op jit(solution)/shard_map/reshape | solution.py:657
  43.3 0.0 copy-done.2
  43.4 1.1 %fusion.4 = f32[64,2,3,8,32]{0,4,3,2,1:T(8,128)S(1)} fusion(f32[4,3,8,32,16]{4,3,2,1,0:T(8,128)S(1)} %reshape.37, f32[4,16,64,2,1,1]{2,1,0,5,4,3:T(8,128)S(1)} %copy-done.2), kind=kOutput, calls=%fused_computation.4 | convolution fusion | flops 37748736 | bytes 622592 | tf_op jit(solution)/shard_map/gcyxz,gzkp->kpcyx/dot_general | solution.py:660
  44.5 0.7 copy.17
  45.2 1.1 %reshape.38.x_ref = f32[8,96,128]{2,1,0:T(8,128)} reshape(f32[64,2,3,8,32]{4,3,2,1,0:T(8,128)S(1)} %copy.17) | data formatting | bytes 786432 | tf_op jit(solution)/shard_map/reshape | solution.py:662
  46.3 13.8 %exchange.1 = (f32[8,96,128]{2,1,0:T(8,128)}, f32[3,40960]{1,0:T(4,128)}) custom-call(s32[3]{0:T(128)} %shift_ref.5, s32[640,128]{1,0:T(8,128)} %bitcast.44, f32[3,81920]{1,0:T(4,128)} %v_ref.5, f32[2,2,6,128,128]{4,3,2,1,0:T(8,128)} %get-tuple-element.10.tab_ref, f32[8,96,128]{2,1,0:T(8,128)} %reshape.38.x_ref), custom_call_target="tpu_custom_call" | custom-call | tf_op jit(solution)/shard_map/exchange/pallas_call | solution.py:475
  60.2 0.0 copy-start.1
  60.2 1.4 %reshape.39 = f32[2,4,8,2,3,8,32]{6,5,4,3,2,1,0:T(8,128)S(1)} reshape(f32[8,96,128]{2,1,0:T(8,128)} %get-tuple-element.13) | data formatting | bytes 786432 | tf_op jit(solution)/shard_map/reshape | solution.py:664
  61.6 0.0 copy-done.1
  61.6 1.4 %fusion.7 = f32[3,8,64,2,32]{2,4,1,0,3:T(8,128)S(1)} fusion(f32[2,2,2,4,8,64,1,1]{5,4,0,6,7,1,3,2:T(8,128)S(1)} %copy-done.1, f32[2,4,8,2,3,8,32]{6,5,4,3,2,1,0:T(8,128)S(1)} %reshape.39), kind=kOutput, calls=%fused_computation.5 | convolution fusion | flops 75497472 | bytes 851968 | tf_op jit(solution)/shard_map/abzpcyx,pqabyk->czkqx/dot_general | solution.py:669
  63.0 0.9 copy.19
  63.9 0.9 reshape.40
  64.8 0.1 copy.20
  64.8 0.3 copy.21
  65.2 0.9 %copy.22.block_ref = f32[4,192,128]{2,1,0:T(8,128)} copy(f32[4,192,128]{1,2,0:T(8,128)S(1)} %bitcast.46) | data formatting | bytes 786432 | tf_op jit(solution)/shard_map/reshape | solution.py:672
  66.1 20.9 %finish.1 = (f32[3,81920]{1,0:T(4,128)}, f32[2,384,128]{2,1,0:T(8,128)}, f32[8,128]{1,0:T(8,128)}) custom-call(s32[3]{0:T(128)} %shift_ref.5, s32[640,128]{1,0:T(8,128)} %bitcast.45, f32[3,81920]{1,0:T(4,128)} %v_ref.5, f32[2,2,6,128,128]{4,3,2,1,0:T(8,128)} %get-tuple-element.10.tab_ref, f32[3,40960]{1,0:T(4,128)} %get-tuple-element.12.done_ref, ...), custom_call_target="tpu_custom_call" | custom-call | tf_op jit(solution)/shard_map/finish/pallas_call | solution.py:611
  87.0 0.0 copy-start
  87.0 1.2 %slice_bitcast_fusion = f32[32]{0:T(128)} fusion(f32[8,128]{1,0:T(8,128)} %get-tuple-element.16), kind=kLoop, calls=%fused_computation.7 | loop fusion | bytes 256 | tf_op jit(solution)/shard_map/squeeze | solution.py:633
  88.3 2.6 %copy.40 = f32[3,81920]{1,0:T(4,128)} copy(f32[3,81920]{1,0:T(4,128)} %get-tuple-element.20) | data formatting | bytes 1966080
  90.9 0.0 copy-done
  90.9 0.7 copy.41
Async XLA Ops:
  17.1 26.2 %copy-start.2 = (f32[4,16,64,2,1,1]{2,1,0,5,4,3:T(8,128)S(1)}, f32[4,16,64,2,1,1]{2,1,0,5,4,3:T(8,128)}, u32[]{:S(2)}) copy-start(f32[4,16,64,2,1,1]{2,1,0,5,4,3:T(8,128)} %constant.12) | copy-start | bytes 98308
  60.2 1.4 %copy-start.1 = (f32[2,2,2,4,8,64,1,1]{5,4,0,6,7,1,3,2:T(8,128)S(1)}, f32[2,2,2,4,8,64,1,1]{5,4,0,6,7,1,3,2:T(8,128)}, u32[]{:S(2)}) copy-start(f32[2,2,2,4,8,64,1,1]{5,4,0,6,7,1,3,2:T(8,128)} %constant.14) | copy-start | bytes 196612
  87.0 3.9 %copy-start = (f32[2,384,128]{2,1,0:T(8,128)S(1)}, f32[2,384,128]{2,1,0:T(8,128)}, u32[]{:S(2)}) copy-start(f32[2,384,128]{2,1,0:T(8,128)} %get-tuple-element.15) | copy-start | bytes 1179652
